TPU v7x, 128 devices: a whole 4x4x4 slice. The times are simulated.
128 devices in a mesh: seq: 64 (over y, z, x_hi, core), head: 2 (over x_lo).
Axes of the slice: x: 4 (x_hi: 2, x_lo: 2; x = x_hi * 2 + x_lo), y: 4, z: 4, core: 2. Of those that a mesh axis runs over, the one named last changes fastest.
Arguments:
- queries: bfloat16 [2, 16384, 2048], P(None, 'seq', 'head'), may hold values from -8 to 8
- key_states: bfloat16 [2, 16384, 2048], P(None, 'seq', 'head'), may hold values from -8 to 8
- value_states: bfloat16 [2, 16384, 2048], P(None, 'seq', 'head'), may hold values from -6 to 6
- output_grad: bfloat16 [2, 16384, 2048], P(None, 'seq', 'head'), may hold values from -6 to 6
- out_proj: bfloat16 [2048, 2048], P('head'), may hold values from -0.125 to 0.125
Outputs:
- layer_out: bfloat16 [2, 16384, 2048], P(None, 'seq', 'head')
- query_grad: bfloat16 [2, 16384, 2048], P(None, 'seq', 'head')
- key_grad: bfloat16 [2, 16384, 2048], P(None, 'seq', 'head')
- value_grad: bfloat16 [2, 16384, 2048], P(None, 'seq', 'head')
All inputs are finite; a program needn't handle non-finite values.
Results may differ from a plain program's by a relative error of at most 0.012.
The roundings to bfloat16 on the way count: a program that leaves them out, or rounds other values in their place, can miss the bound.
Values may be sent and summed in bfloat16 or wider, within the bound.
A program may use at most 192 MiB of HBM per device.

v0:
```python
from functools import partial

import jax
import jax.numpy as jnp
from jax import lax
from jax.sharding import PartitionSpec as P

HEAD_DIM = 128


def passed_along(shard, axis, by):
    length = lax.axis_size(axis)
    pairs = [(i, i + by) for i in range(length) if 0 <= i + by < length]
    return lax.ppermute(shard, axis, pairs)


def head_major(source):
    batch_rows, token_rows, features = source.shape
    return jnp.transpose(
        source.reshape(batch_rows, token_rows, features // HEAD_DIM, HEAD_DIM), (2, 0, 1, 3)
    )


def row_major(source):
    head_count, batch_rows, token_rows, features = source.shape
    return jnp.transpose(source, (1, 2, 0, 3)).reshape(
        batch_rows, token_rows, head_count * features
    )


def head_pass(pieces, key_mask, score_scale, whole):
    query_row_block, key_row_block, value_row_block, gradient_row_block = pieces
    own_rows = query_row_block.shape[1]
    scores = (
        jnp.einsum(
            "xei,xgi->xeg", query_row_block, key_row_block, preferred_element_type=jnp.float32
        )
        * score_scale
    )
    scores = jnp.where(key_mask, scores, -jnp.inf)
    maxima = jnp.max(scores, axis=2, keepdims=True)
    log_norm = maxima + jnp.log(jnp.sum(jnp.exp(scores - maxima), axis=2, keepdims=True))
    weights = jnp.exp(scores - log_norm)
    lower_weight_block = weights.astype(jnp.bfloat16)
    attn_block = jnp.einsum(
        "ifj,ijx->ifx", lower_weight_block, value_row_block, preferred_element_type=jnp.float32
    ).astype(jnp.bfloat16)
    row_dsum = jnp.sum(
        gradient_row_block.astype(jnp.float32) * attn_block.astype(jnp.float32),
        axis=2,
        keepdims=True,
    )
    grad_weights = jnp.einsum(
        "xei,xgi->xeg", gradient_row_block, value_row_block, preferred_element_type=jnp.float32
    )
    score_gradients = (weights * (grad_weights - row_dsum)).astype(jnp.bfloat16)
    dquery = (
        jnp.einsum(
            "ifj,ijx->ifx", score_gradients, key_row_block, preferred_element_type=jnp.float32
        )
        * score_scale
    ).astype(jnp.bfloat16)
    key_term = (
        jnp.einsum(
            "uwp,uwf->upf", score_gradients, query_row_block, preferred_element_type=jnp.float32
        )
        * score_scale
    )
    value_term = jnp.einsum(
        "uwp,uwf->upf", lower_weight_block, gradient_row_block, preferred_element_type=jnp.float32
    )
    return (
        attn_block,
        dquery,
        key_term[:, :own_rows],
        value_term[:, :own_rows],
        key_term[:, own_rows:].astype(jnp.bfloat16),
        value_term[:, own_rows:].astype(jnp.bfloat16),
    )


def body(queries, key_states, value_states, output_grad, out_proj):
    score_scale = HEAD_DIM ** (-0.5)
    levels = lax.axis_size("seq").bit_length() - 1
    seq_place = lax.axis_index("seq")
    own_rows = queries.shape[1]
    attn_grad = jnp.einsum(
        "brf,df->brd",
        lax.all_gather(output_grad, "head", axis=2, tiled=True),
        out_proj,
        preferred_element_type=jnp.float32,
    ).astype(jnp.bfloat16)
    causal = jnp.arange(own_rows)[:, None] >= jnp.arange(own_rows)[None, :]
    partner_flags = [seq_place // 2**bit_index % 2 == 1 for bit_index in range(levels)]
    key_mask = jnp.concatenate(
        [causal]
        + [jnp.broadcast_to(flag_value, (own_rows, own_rows)) for flag_value in partner_flags],
        axis=1,
    )
    key_parts = [key_states]
    value_parts = [value_states]
    for bit_index in range(levels):
        far_key, far_value = passed_along((key_states, value_states), "seq", 2**bit_index)
        key_parts.append(far_key)
        value_parts.append(far_value)
    pieces = (
        head_major(queries),
        head_major(jnp.concatenate(key_parts, axis=1)),
        head_major(jnp.concatenate(value_parts, axis=1)),
        head_major(attn_grad),
    )
    attn_heads, dquery_heads, own_key, own_value, far_keys, far_values = lax.map(
        partial(head_pass, key_mask=key_mask, score_scale=score_scale, whole=True), pieces
    )
    key_total = row_major(own_key)
    value_total = row_major(own_value)
    for bit_index in range(levels):
        low = bit_index * own_rows
        sent_key = row_major(far_keys[:, :, low : low + own_rows])
        sent_value = row_major(far_values[:, :, low : low + own_rows])
        back_key, back_value = passed_along((sent_key, sent_value), "seq", -(2**bit_index))
        key_total = key_total + back_key.astype(jnp.float32)
        value_total = value_total + back_value.astype(jnp.float32)
    attn_rows = row_major(attn_heads)
    query_grad = row_major(dquery_heads)
    partial_out = jnp.einsum("brd,df->brf", attn_rows, out_proj, preferred_element_type=jnp.float32)
    layer_out = lax.psum_scatter(partial_out, "head", scatter_dimension=2, tiled=True).astype(
        jnp.bfloat16
    )
    return (layer_out, query_grad, key_total.astype(jnp.bfloat16), value_total.astype(jnp.bfloat16))


def solution(mesh):
    in_specs = (
        P(None, "seq", "head"),
        P(None, "seq", "head"),
        P(None, "seq", "head"),
        P(None, "seq", "head"),
        P("head", None),
    )
    out_specs = (
        P(None, "seq", "head"),
        P(None, "seq", "head"),
        P(None, "seq", "head"),
        P(None, "seq", "head"),
    )
    return jax.shard_map(body, mesh=mesh, in_specs=in_specs, out_specs=out_specs, check_vma=False)
```

profile of v0, /device:TPU:14, one launch (start us, length us, event | category | flops | bytes accessed | tf_op | source)
XLA Modules:
  0.0 656.2 jit_solution(15053760238046626793)
XLA Ops:
  8.8 5.2 collective-permute-start.11
  15.9 5.8 collective-permute-start.9
  21.7 3.8 collective-permute-start.7
  27.6 7.8 %collective-permute-done.11 = bf16[2,256,1024]{1,2,0:T(8,128)(2,1)} collective-permute-done((bf16[2,256,1024]{1,2,0:T(8,128)(2,1)S(1)}, bf16[2,256,1024]{1,2,0:T(8,128)(2,1)}, u32[]{:S(2)}, u32[]{:S(2)}) %collective-permute-start.11) | collective-permute-done | bytes 1048608 | tf_op jit(solution)/shard_map/ppermute | solution.py:14
  35.4 3.8 collective-permute-start.8
  40.6 19.2 %collective-permute-done.10 = bf16[2,256,1024]{1,2,0:T(8,128)(2,1)} collective-permute-done((bf16[2,256,1024]{1,2,0:T(8,128)(2,1)S(1)}, bf16[2,256,1024]{1,2,0:T(8,128)(2,1)}, u32[]{:S(2)}, u32[]{:S(2)}) %collective-permute-start.10) | collective-permute-done | bytes 1048608 | tf_op jit(solution)/shard_map/ppermute | solution.py:14
  65.9 20.3 %collective-permute-done.9 = bf16[2,256,1024]{1,2,0:T(8,128)(2,1)} collective-permute-done((bf16[2,256,1024]{1,2,0:T(8,128)(2,1)S(1)}, bf16[2,256,1024]{1,2,0:T(8,128)(2,1)}, u32[]{:S(2)}, u32[]{:S(2)}) %collective-permute-start.9) | collective-permute-done | bytes 1048608 | tf_op jit(solution)/shard_map/ppermute | solution.py:14
  86.2 72.5 %collective-permute-start.1 = (bf16[2,256,1024]{1,2,0:T(8,128)(2,1)}, bf16[2,256,1024]{1,2,0:T(8,128)(2,1)S(1)}, u32[]{:S(2)}, u32[]{:S(2)}) collective-permute-start(bf16[2,256,1024]{1,2,0:T(8,128)(2,1)} %copy.43), channel_id=1, source_target_pairs={{0,4},{2,6},{4,8},{6,10},{8,12},{10,14},{12,16},{14,18},{16,20},{1... | collective-permute-start | bytes 3145736 | tf_op jit(solution)/shard_map/ppermute | solution.py:14
  173.9 3.3 constant_dynamic-update-slice_fusion.5
  180.5 27.5 %collective-permute-done.2 = bf16[2,256,1024]{1,2,0:T(8,128)(2,1)S(1)} collective-permute-done((bf16[2,256,1024]{1,2,0:T(8,128)(2,1)}, bf16[2,256,1024]{1,2,0:T(8,128)(2,1)S(1)}, u32[]{:S(2)}, u32[]{:S(2)}) %collective-permute-start.2) | collective-permute-done | bytes 1048608 | tf_op jit(solution)/shard_map/ppermute | solution.py:14
  212.6 5.2 fusion.51
  220.7 115.5 %while.20 = (s32[]{:T(128)}, bf16[8,2,256,128]{2,3,0,1:T(8,128)(2,1)}, bf16[8,2,256,128]{3,2,1,0:T(8,128)(2,1)}, f32[8,2,256,128]{3,2,1,0:T(8,128)}, f32[8,2,256...) while((s32[]{:T(128)}, ...), condition=%wide.region_4.5_spmd, body=%wide.region_0.4_spmd.sunk | while | flops 1422130176 | bytes 37054616 | solution.py:112
  336.1 6.8 %fusion.35 = f32[2,256,2048]{2,1,0:T(8,128)} fusion(bf16[2,256,1024]{1,2,0:T(8,128)(2,1)} %bitcast.233, bf16[1024,2048]{1,0:T(8,128)(2,1)} %param.11), kind=kOutput, calls=%fused_computation.47 | convolution fusion | flops 2147483648 | bytes 9437184 | tf_op jit(solution)/shard_map/brd,df->brf/dot_general | solution.py:126
  343.0 5.4 slice_bitcast_fusion.7
  348.7 26.5 %collective-permute-start.12 = (bf16[2,256,1024]{2,1,0:T(8,128)(2,1)S(1)}, bf16[2,256,1024]{2,1,0:T(8,128)(2,1)S(1)}, u32[]{:S(2)}, u32[]{:S(2)}) collective-permute-start(bf16[2,256,1024]{2,1,0:T(8,128)(2,1)S(1)} %bitcast.245), channel_id=1, source_target_pairs={{2,0},{4,2},{6,4},{8,6},{10,8},{12,10},{14,12},{16,14},{18,16},{20... | collective-permute-start | bytes 3145736 | tf_op jit(solution)/shard_map/ppermute | solution.py:14
  380.1 17.5 %collective-permute-start.15 = (bf16[2,256,1024]{2,1,0:T(8,128)(2,1)S(1)}, bf16[2,256,1024]{2,1,0:T(8,128)(2,1)S(1)}, u32[]{:S(2)}, u32[]{:S(2)}) collective-permute-start(bf16[2,256,1024]{2,1,0:T(8,128)(2,1)S(1)} %bitcast.240), channel_id=1, source_target_pairs={{16,0},{18,2},{20,4},{22,6},{24,8},{26,10},{28,12},{30,14},{32,16}... | collective-permute-start | bytes 3145736 | tf_op jit(solution)/shard_map/ppermute | solution.py:14
  397.9 37.9 %collective-permute-start.14 = (bf16[2,256,1024]{2,1,0:T(8,128)(2,1)S(1)}, bf16[2,256,1024]{2,1,0:T(8,128)(2,1)S(1)}, u32[]{:S(2)}, u32[]{:S(2)}) collective-permute-start(bf16[2,256,1024]{2,1,0:T(8,128)(2,1)S(1)} %bitcast.242), channel_id=1, source_target_pairs={{8,0},{10,2},{12,4},{14,6},{16,8},{18,10},{20,12},{22,14},{24,16},... | collective-permute-start | bytes 3145736 | tf_op jit(solution)/shard_map/ppermute | solution.py:14
  435.8 3.3 collective-permute-start.13
  439.2 29.1 %collective-permute-start.19 = (bf16[2,256,1024]{2,1,0:T(8,128)(2,1)S(1)}, bf16[2,256,1024]{2,1,0:T(8,128)(2,1)S(1)}, u32[]{:S(2)}, u32[]{:S(2)}) collective-permute-start(bf16[2,256,1024]{2,1,0:T(8,128)(2,1)S(1)} %bitcast.234), channel_id=1, source_target_pairs={{4,0},{6,2},{8,4},{10,6},{12,8},{14,10},{16,12},{18,14},{20,16},{2... | collective-permute-start | bytes 3145736 | tf_op jit(solution)/shard_map/ppermute | solution.py:14
  473.7 80.3 %collective-permute-done.14 = bf16[2,256,1024]{2,1,0:T(8,128)(2,1)S(1)} collective-permute-done((bf16[2,256,1024]{2,1,0:T(8,128)(2,1)S(1)}, bf16[2,256,1024]{2,1,0:T(8,128)(2,1)S(1)}, u32[]{:S(2)}, u32[]{:S(2)}) %collective-permute-start.14) | collective-permute-done | bytes 1048608 | tf_op jit(solution)/shard_map/ppermute | solution.py:14
  562.9 10.1 %collective-permute-done.20 = bf16[2,256,1024]{2,1,0:T(8,128)(2,1)S(1)} collective-permute-done((bf16[2,256,1024]{2,1,0:T(8,128)(2,1)S(1)}, bf16[2,256,1024]{2,1,0:T(8,128)(2,1)S(1)}, u32[]{:S(2)}, u32[]{:S(2)}) %collective-permute-start.20) | collective-permute-done | bytes 1048608 | tf_op jit(solution)/shard_map/ppermute | solution.py:14
  573.1 22.5 %collective-permute-done.21 = bf16[2,256,1024]{2,1,0:T(8,128)(2,1)S(1)} collective-permute-done((bf16[2,256,1024]{2,1,0:T(8,128)(2,1)S(1)}, bf16[2,256,1024]{2,1,0:T(8,128)(2,1)S(1)}, u32[]{:S(2)}, u32[]{:S(2)}) %collective-permute-start.21) | collective-permute-done | bytes 1048608 | tf_op jit(solution)/shard_map/ppermute | solution.py:14
  595.6 27.8 %collective-permute-done.22 = bf16[2,256,1024]{2,1,0:T(8,128)(2,1)S(1)} collective-permute-done((bf16[2,256,1024]{2,1,0:T(8,128)(2,1)S(1)}, bf16[2,256,1024]{2,1,0:T(8,128)(2,1)S(1)}, u32[]{:S(2)}, u32[]{:S(2)}) %collective-permute-start.22) | collective-permute-done | bytes 1048608 | tf_op jit(solution)/shard_map/ppermute | solution.py:14
  623.4 20.8 %collective-permute-done.23 = bf16[2,256,1024]{2,1,0:T(8,128)(2,1)S(1)} collective-permute-done((bf16[2,256,1024]{2,1,0:T(8,128)(2,1)S(1)}, bf16[2,256,1024]{2,1,0:T(8,128)(2,1)S(1)}, u32[]{:S(2)}, u32[]{:S(2)}) %collective-permute-start.23) | collective-permute-done | bytes 1048608 | tf_op jit(solution)/shard_map/ppermute | solution.py:14
  (180 shorter events, 178.9 us)
Async XLA Ops:
  7.2 205.4 %all-gather.2.cloned.1.call-start = ((), (), s32[]{:S(2)}) async-start(), calls=%async_computation.1 | async-start | bytes 3145728 | tf_op jit(solution)/shard_map/all_gather | solution.py:89
  14.0 45.8 %collective-permute-start.10 = (bf16[2,256,1024]{1,2,0:T(8,128)(2,1)S(1)}, bf16[2,256,1024]{1,2,0:T(8,128)(2,1)}, u32[]{:S(2)}, u32[]{:S(2)}) collective-permute-start(bf16[2,256,1024]{1,2,0:T(8,128)(2,1)S(1)} %copy.50), channel_id=1, source_target_pairs={{0,32},{2,34},{4,36},{6,38},{8,40},{10,42},{12,44},{14,46},{16,48}... | collective-permute-start | bytes 3145736 | tf_op jit(solution)/shard_map/ppermute | solution.py:14
  15.9 70.3 %collective-permute-start.9 = (bf16[2,256,1024]{1,2,0:T(8,128)(2,1)S(1)}, bf16[2,256,1024]{1,2,0:T(8,128)(2,1)}, u32[]{:S(2)}, u32[]{:S(2)}) collective-permute-start(bf16[2,256,1024]{1,2,0:T(8,128)(2,1)S(1)} %copy.50), channel_id=1, source_target_pairs={{0,16},{2,18},{4,20},{6,22},{8,24},{10,26},{12,28},{14,30},{16,32}... | collective-permute-start | bytes 3145736 | tf_op jit(solution)/shard_map/ppermute | solution.py:14
  21.7 140.3 %collective-permute-start.7 = (bf16[2,256,1024]{1,2,0:T(8,128)(2,1)S(1)}, bf16[2,256,1024]{1,2,0:T(8,128)(2,1)}, u32[]{:S(2)}, u32[]{:S(2)}) collective-permute-start(bf16[2,256,1024]{1,2,0:T(8,128)(2,1)S(1)} %copy.50), channel_id=1, source_target_pairs={{0,4},{2,6},{4,8},{6,10},{8,12},{10,14},{12,16},{14,18},{16,20},{1... | collective-permute-start | bytes 3145736 | tf_op jit(solution)/shard_map/ppermute | solution.py:14
  25.5 133.3 %collective-permute-start.6 = (bf16[2,256,1024]{1,2,0:T(8,128)(2,1)S(1)}, bf16[2,256,1024]{1,2,0:T(8,128)(2,1)}, u32[]{:S(2)}, u32[]{:S(2)}) collective-permute-start(bf16[2,256,1024]{1,2,0:T(8,128)(2,1)S(1)} %copy.50), channel_id=1, source_target_pairs={{0,2},{2,4},{4,6},{6,8},{8,10},{10,12},{12,14},{14,16},{16,18},{18... | collective-permute-start | bytes 3145736 | tf_op jit(solution)/shard_map/ppermute | solution.py:14
  27.4 619.2 %reduce-scatter.2.cloned.1.call-start = ((), (), s32[]{:S(2)}) async-start(), calls=%async_computation.2 | async-start | bytes 6291456 | tf_op jit(solution)/shard_map/reduce_scatter | solution.py:127
  35.4 129.8 %collective-permute-start.8 = (bf16[2,256,1024]{1,2,0:T(8,128)(2,1)S(1)}, bf16[2,256,1024]{1,2,0:T(8,128)(2,1)}, u32[]{:S(2)}, u32[]{:S(2)}) collective-permute-start(bf16[2,256,1024]{1,2,0:T(8,128)(2,1)S(1)} %copy.50), channel_id=1, source_target_pairs={{0,8},{2,10},{4,12},{6,14},{8,16},{10,18},{12,20},{14,22},{16,24},... | collective-permute-start | bytes 3145736 | tf_op jit(solution)/shard_map/ppermute | solution.py:14
  59.8 108.6 %collective-permute-start = (bf16[2,256,1024]{1,2,0:T(8,128)(2,1)}, bf16[2,256,1024]{1,2,0:T(8,128)(2,1)}, u32[]{:S(2)}, u32[]{:S(2)}) collective-permute-start(bf16[2,256,1024]{1,2,0:T(8,128)(2,1)} %copy.43), channel_id=1, source_target_pairs={{0,2},{2,4},{4,6},{6,8},{8,10},{10,12},{12,14},{14,16},{16,18},{18... | collective-permute-start | bytes 3145736 | tf_op jit(solution)/shard_map/ppermute | solution.py:14
  86.2 93.2 %collective-permute-start.1 = (bf16[2,256,1024]{1,2,0:T(8,128)(2,1)}, bf16[2,256,1024]{1,2,0:T(8,128)(2,1)S(1)}, u32[]{:S(2)}, u32[]{:S(2)}) collective-permute-start(bf16[2,256,1024]{1,2,0:T(8,128)(2,1)} %copy.43), channel_id=1, source_target_pairs={{0,4},{2,6},{4,8},{6,10},{8,12},{10,14},{12,16},{14,18},{16,20},{1... | collective-permute-start | bytes 3145736 | tf_op jit(solution)/shard_map/ppermute | solution.py:14
  158.7 49.3 %collective-permute-start.2 = (bf16[2,256,1024]{1,2,0:T(8,128)(2,1)}, bf16[2,256,1024]{1,2,0:T(8,128)(2,1)S(1)}, u32[]{:S(2)}, u32[]{:S(2)}) collective-permute-start(bf16[2,256,1024]{1,2,0:T(8,128)(2,1)} %copy.43), channel_id=1, source_target_pairs={{0,8},{2,10},{4,12},{6,14},{8,16},{10,18},{12,20},{14,22},{16,24},... | collective-permute-start | bytes 3145736 | tf_op jit(solution)/shard_map/ppermute | solution.py:14
  162.0 47.2 %collective-permute-start.3 = (bf16[2,256,1024]{1,2,0:T(8,128)(2,1)}, bf16[2,256,1024]{1,2,0:T(8,128)(2,1)S(1)}, u32[]{:S(2)}, u32[]{:S(2)}) collective-permute-start(bf16[2,256,1024]{1,2,0:T(8,128)(2,1)} %copy.43), channel_id=1, source_target_pairs={{0,16},{2,18},{4,20},{6,22},{8,24},{10,26},{12,28},{14,30},{16,32}... | collective-permute-start | bytes 3145736 | tf_op jit(solution)/shard_map/ppermute | solution.py:14
  165.2 45.1 %collective-permute-start.4 = (bf16[2,256,1024]{1,2,0:T(8,128)(2,1)}, bf16[2,256,1024]{1,2,0:T(8,128)(2,1)S(1)}, u32[]{:S(2)}, u32[]{:S(2)}) collective-permute-start(bf16[2,256,1024]{1,2,0:T(8,128)(2,1)} %copy.43), channel_id=1, source_target_pairs={{0,32},{2,34},{4,36},{6,38},{8,40},{10,42},{12,44},{14,46},{16,48}... | collective-permute-start | bytes 3145736 | tf_op jit(solution)/shard_map/ppermute | solution.py:14
  348.7 87.1 %collective-permute-start.12 = (bf16[2,256,1024]{2,1,0:T(8,128)(2,1)S(1)}, bf16[2,256,1024]{2,1,0:T(8,128)(2,1)S(1)}, u32[]{:S(2)}, u32[]{:S(2)}) collective-permute-start(bf16[2,256,1024]{2,1,0:T(8,128)(2,1)S(1)} %bitcast.245), channel_id=1, source_target_pairs={{2,0},{4,2},{6,4},{8,6},{10,8},{12,10},{14,12},{16,14},{18,16},{20... | collective-permute-start | bytes 3145736 | tf_op jit(solution)/shard_map/ppermute | solution.py:14
  375.5 63.7 %collective-permute-start.17 = (bf16[2,256,1024]{2,1,0:T(8,128)(2,1)S(1)}, bf16[2,256,1024]{2,1,0:T(8,128)(2,1)S(1)}, u32[]{:S(2)}, u32[]{:S(2)}) collective-permute-start(bf16[2,256,1024]{2,1,0:T(8,128)(2,1)S(1)} %bitcast.244), channel_id=1, source_target_pairs={{64,0},{66,2},{68,4},{70,6},{72,8},{74,10},{76,12},{78,14},{80,16}... | collective-permute-start | bytes 3145736 | tf_op jit(solution)/shard_map/ppermute | solution.py:14
  378.2 91.5 %collective-permute-start.16 = (bf16[2,256,1024]{2,1,0:T(8,128)(2,1)S(1)}, bf16[2,256,1024]{2,1,0:T(8,128)(2,1)S(1)}, u32[]{:S(2)}, u32[]{:S(2)}) collective-permute-start(bf16[2,256,1024]{2,1,0:T(8,128)(2,1)S(1)} %bitcast.243), channel_id=1, source_target_pairs={{32,0},{34,2},{36,4},{38,6},{40,8},{42,10},{44,12},{46,14},{48,16}... | collective-permute-start | bytes 3145736 | tf_op jit(solution)/shard_map/ppermute | solution.py:14
  380.1 91.7 %collective-permute-start.15 = (bf16[2,256,1024]{2,1,0:T(8,128)(2,1)S(1)}, bf16[2,256,1024]{2,1,0:T(8,128)(2,1)S(1)}, u32[]{:S(2)}, u32[]{:S(2)}) collective-permute-start(bf16[2,256,1024]{2,1,0:T(8,128)(2,1)S(1)} %bitcast.240), channel_id=1, source_target_pairs={{16,0},{18,2},{20,4},{22,6},{24,8},{26,10},{28,12},{30,14},{32,16}... | collective-permute-start | bytes 3145736 | tf_op jit(solution)/shard_map/ppermute | solution.py:14
  397.9 156.2 %collective-permute-start.14 = (bf16[2,256,1024]{2,1,0:T(8,128)(2,1)S(1)}, bf16[2,256,1024]{2,1,0:T(8,128)(2,1)S(1)}, u32[]{:S(2)}, u32[]{:S(2)}) collective-permute-start(bf16[2,256,1024]{2,1,0:T(8,128)(2,1)S(1)} %bitcast.242), channel_id=1, source_target_pairs={{8,0},{10,2},{12,4},{14,6},{16,8},{18,10},{20,12},{22,14},{24,16},... | collective-permute-start | bytes 3145736 | tf_op jit(solution)/shard_map/ppermute | solution.py:14
  435.8 120.2 %collective-permute-start.13 = (bf16[2,256,1024]{2,1,0:T(8,128)(2,1)S(1)}, bf16[2,256,1024]{2,1,0:T(8,128)(2,1)S(1)}, u32[]{:S(2)}, u32[]{:S(2)}) collective-permute-start(bf16[2,256,1024]{2,1,0:T(8,128)(2,1)S(1)} %bitcast.236), channel_id=1, source_target_pairs={{4,0},{6,2},{8,4},{10,6},{12,8},{14,10},{16,12},{18,14},{20,16},{2... | collective-permute-start | bytes 3145736 | tf_op jit(solution)/shard_map/ppermute | solution.py:14
  439.2 118.1 %collective-permute-start.19 = (bf16[2,256,1024]{2,1,0:T(8,128)(2,1)S(1)}, bf16[2,256,1024]{2,1,0:T(8,128)(2,1)S(1)}, u32[]{:S(2)}, u32[]{:S(2)}) collective-permute-start(bf16[2,256,1024]{2,1,0:T(8,128)(2,1)S(1)} %bitcast.234), channel_id=1, source_target_pairs={{4,0},{6,2},{8,4},{10,6},{12,8},{14,10},{16,12},{18,14},{20,16},{2... | collective-permute-start | bytes 3145736 | tf_op jit(solution)/shard_map/ppermute | solution.py:14
  469.7 103.4 %collective-permute-start.20 = (bf16[2,256,1024]{2,1,0:T(8,128)(2,1)S(1)}, bf16[2,256,1024]{2,1,0:T(8,128)(2,1)S(1)}, u32[]{:S(2)}, u32[]{:S(2)}) collective-permute-start(bf16[2,256,1024]{2,1,0:T(8,128)(2,1)S(1)} %bitcast.241), channel_id=1, source_target_pairs={{8,0},{10,2},{12,4},{14,6},{16,8},{18,10},{20,12},{22,14},{24,16},... | collective-permute-start | bytes 3145736 | tf_op jit(solution)/shard_map/ppermute | solution.py:14
  471.8 123.8 %collective-permute-start.21 = (bf16[2,256,1024]{2,1,0:T(8,128)(2,1)S(1)}, bf16[2,256,1024]{2,1,0:T(8,128)(2,1)S(1)}, u32[]{:S(2)}, u32[]{:S(2)}) collective-permute-start(bf16[2,256,1024]{2,1,0:T(8,128)(2,1)S(1)} %bitcast.239), channel_id=1, source_target_pairs={{16,0},{18,2},{20,4},{22,6},{24,8},{26,10},{28,12},{30,14},{32,16}... | collective-permute-start | bytes 3145736 | tf_op jit(solution)/shard_map/ppermute | solution.py:14
  554.0 69.3 %collective-permute-start.22 = (bf16[2,256,1024]{2,1,0:T(8,128)(2,1)S(1)}, bf16[2,256,1024]{2,1,0:T(8,128)(2,1)S(1)}, u32[]{:S(2)}, u32[]{:S(2)}) collective-permute-start(bf16[2,256,1024]{2,1,0:T(8,128)(2,1)S(1)} %bitcast.238), channel_id=1, source_target_pairs={{32,0},{34,2},{36,4},{38,6},{40,8},{42,10},{44,12},{46,14},{48,16}... | collective-permute-start | bytes 3145736 | tf_op jit(solution)/shard_map/ppermute | solution.py:14
  556.0 88.2 %collective-permute-start.23 = (bf16[2,256,1024]{2,1,0:T(8,128)(2,1)S(1)}, bf16[2,256,1024]{2,1,0:T(8,128)(2,1)S(1)}, u32[]{:S(2)}, u32[]{:S(2)}) collective-permute-start(bf16[2,256,1024]{2,1,0:T(8,128)(2,1)S(1)} %bitcast.237), channel_id=1, source_target_pairs={{64,0},{66,2},{68,4},{70,6},{72,8},{74,10},{76,12},{78,14},{80,16}... | collective-permute-start | bytes 3145736 | tf_op jit(solution)/shard_map/ppermute | solution.py:14
  557.3 86.9 %collective-permute-start.18 = (bf16[2,256,1024]{2,1,0:T(8,128)(2,1)S(1)}, bf16[2,256,1024]{2,1,0:T(8,128)(2,1)S(1)}, u32[]{:S(2)}, u32[]{:S(2)}) collective-permute-start(bf16[2,256,1024]{2,1,0:T(8,128)(2,1)S(1)} %bitcast.235), channel_id=1, source_target_pairs={{2,0},{4,2},{6,4},{8,6},{10,8},{12,10},{14,12},{16,14},{18,16},{20... | collective-permute-start | bytes 3145736 | tf_op jit(solution)/shard_map/ppermute | solution.py:14
  (7 other events, 403.6 us)
Sparse Core Ops, SparseCore 0:
  27.5 51.8 all-gather.1
  343.1 162.7 reduce-scatter.1
where the time goes:
time: 659 us; the launch traced here: 656 us
  waiting for transfers between devices  239 us (36%)
  starting transfers between devices  231 us (35%)
  matrix products  103 us (16%)
  local copies, waits for them, and re-layouts  54.9 us (8%)
  between operations  14.8 us (2%)
  other arithmetic  13.5 us (2%)
    ppermute x24, waiting for transfers between devices, passed_along(): return lax.ppermute(shard, axis, pairs)  239 us
    ppermute x24, starting transfers between devices, passed_along(): return lax.ppermute(shard, axis, pairs)  231 us
    unnamed x32, local copies, waits for them, and re-layouts  27.9 us
    dot_general x8, matrix products, head_pass(): jnp.einsum('ifj,ijx->ifx', lower_weight_block, value_row_block, preferred...  21.6 us
    dot_general x8, matrix products, head_pass(): jnp.einsum('ifj,ijx->ifx', score_gradients, key_row_block, preferred_elem...  19.9 us
    dynamic_update_slice x16, local copies, waits for them, and re-layouts, body(): lax.map(partial(head_pass, key_mask=key_mask, score_scale=score_scale, wh...  18.4 us
    dot_general x8, matrix products, head_pass(): jnp.einsum('xei,xgi->xeg', gradient_row_block, value_row_block, preferred...  17.5 us
    dot_general x8, matrix products, head_pass(): jnp.einsum('xei,xgi->xeg', query_row_block, key_row_block, preferred_elem...  17.2 us
  transfers between devices with their start and end apart: 26, of which 10 were waited for; matrix products, arithmetic and copies ran while one was open for 6% of the time, Pallas kernels for 0%

commit v1 on v0

--- a/solution.py
+++ b/solution.py
@@ -10,7 +10,7 @@
 
 def passed_along(shard, axis, by):
     length = lax.axis_size(axis)
-    pairs = [(i, i + by) for i in range(length) if 0 <= i + by < length]
+    pairs = [(i, i ^ abs(by)) for i in range(length) if ((i & abs(by)) == 0) == (by > 0)]
     return lax.ppermute(shard, axis, pairs)
 
 

time: 659 us -> 386 us (0.59)
  the two profiles are of different devices: /device:TPU:14 before, /device:TPU:72 now
where the time goes in v1:
time: 386 us; the launch traced here: 383 us
  waiting for transfers between devices  131 us (34%)
  matrix products  103 us (27%)
  starting transfers between devices  66.2 us (17%)
  local copies, waits for them, and re-layouts  54.9 us (14%)
  between operations  14.7 us (4%)
  other arithmetic  13.5 us (3%)
    ppermute x24, waiting for transfers between devices, passed_along(): return lax.ppermute(shard, axis, pairs)  131 us
    ppermute x24, starting transfers between devices, passed_along(): return lax.ppermute(shard, axis, pairs)  66.1 us
    unnamed x32, local copies, waits for them, and re-layouts  27.9 us
    dot_general x8, matrix products, head_pass(): jnp.einsum('ifj,ijx->ifx', lower_weight_block, value_row_block, preferred...  21.6 us
    dot_general x8, matrix products, head_pass(): jnp.einsum('ifj,ijx->ifx', score_gradients, key_row_block, preferred_elem...  19.9 us
    dynamic_update_slice x16, local copies, waits for them, and re-layouts, body(): lax.map(partial(head_pass, key_mask=key_mask, score_scale=score_scale, wh...  18.4 us
    dot_general x8, matrix products, head_pass(): jnp.einsum('xei,xgi->xeg', gradient_row_block, value_row_block, preferred...  17.5 us
    dot_general x8, matrix products, head_pass(): jnp.einsum('xei,xgi->xeg', query_row_block, key_row_block, preferred_elem...  17.2 us
  transfers between devices with their start and end apart: 26, of which 12 were waited for; matrix products, arithmetic and copies ran while one was open for 10% of the time, Pallas kernels for 0%

profile of v1, /device:TPU:72, one launch (start us, length us, event | category | flops | bytes accessed | tf_op | source)
XLA Modules:
  0.0 383.3 jit_solution(15330808488872411540)
XLA Ops:
  8.8 5.2 %collective-permute-start.11 = (bf16[2,256,1024]{1,2,0:T(8,128)(2,1)S(1)}, bf16[2,256,1024]{1,2,0:T(8,128)(2,1)}, u32[]{:S(2)}, u32[]{:S(2)}) collective-permute-start(bf16[2,256,1024]{1,2,0:T(8,128)(2,1)S(1)} %copy.50), channel_id=1, source_target_pairs={{0,64},{2,66},{4,68},{6,70},{8,72},{10,74},{12,76},{14,78},{16,80}... | collective-permute-start | bytes 3145736 | tf_op jit(solution)/shard_map/ppermute | solution.py:14
  16.6 5.9 %collective-permute-start.7 = (bf16[2,256,1024]{1,2,0:T(8,128)(2,1)S(1)}, bf16[2,256,1024]{1,2,0:T(8,128)(2,1)}, u32[]{:S(2)}, u32[]{:S(2)}) collective-permute-start(bf16[2,256,1024]{1,2,0:T(8,128)(2,1)S(1)} %copy.50), channel_id=1, source_target_pairs={{0,4},{2,6},{8,12},{10,14},{16,20},{18,22},{24,28},{26,30},{32,36}... | collective-permute-start | bytes 3145736 | tf_op jit(solution)/shard_map/ppermute | solution.py:14
  24.9 10.4 %collective-permute-done.11 = bf16[2,256,1024]{1,2,0:T(8,128)(2,1)} collective-permute-done((bf16[2,256,1024]{1,2,0:T(8,128)(2,1)S(1)}, bf16[2,256,1024]{1,2,0:T(8,128)(2,1)}, u32[]{:S(2)}, u32[]{:S(2)}) %collective-permute-start.11) | collective-permute-done | bytes 1048608 | tf_op jit(solution)/shard_map/ppermute | solution.py:14
  35.4 4.5 %collective-permute-start.8 = (bf16[2,256,1024]{1,2,0:T(8,128)(2,1)S(1)}, bf16[2,256,1024]{1,2,0:T(8,128)(2,1)}, u32[]{:S(2)}, u32[]{:S(2)}) collective-permute-start(bf16[2,256,1024]{1,2,0:T(8,128)(2,1)S(1)} %copy.50), channel_id=1, source_target_pairs={{0,8},{2,10},{4,12},{6,14},{16,24},{18,26},{20,28},{22,30},{32,40}... | collective-permute-start | bytes 3145736 | tf_op jit(solution)/shard_map/ppermute | solution.py:14
  41.3 18.5 %collective-permute-done.10 = bf16[2,256,1024]{1,2,0:T(8,128)(2,1)} collective-permute-done((bf16[2,256,1024]{1,2,0:T(8,128)(2,1)S(1)}, bf16[2,256,1024]{1,2,0:T(8,128)(2,1)}, u32[]{:S(2)}, u32[]{:S(2)}) %collective-permute-start.10) | collective-permute-done | bytes 1048608 | tf_op jit(solution)/shard_map/ppermute | solution.py:14
  66.2 5.0 %collective-permute-start.1 = (bf16[2,256,1024]{1,2,0:T(8,128)(2,1)}, bf16[2,256,1024]{1,2,0:T(8,128)(2,1)S(1)}, u32[]{:S(2)}, u32[]{:S(2)}) collective-permute-start(bf16[2,256,1024]{1,2,0:T(8,128)(2,1)} %copy.43), channel_id=1, source_target_pairs={{0,4},{2,6},{8,12},{10,14},{16,20},{18,22},{24,28},{26,30},{32,36}... | collective-permute-start | bytes 3145736 | tf_op jit(solution)/shard_map/ppermute | solution.py:14
  71.3 3.6 collective-permute-start.2
  86.8 3.3 constant_dynamic-update-slice_fusion.5
  96.5 21.7 %collective-permute-done.3 = bf16[2,256,1024]{1,2,0:T(8,128)(2,1)S(1)} collective-permute-done((bf16[2,256,1024]{1,2,0:T(8,128)(2,1)}, bf16[2,256,1024]{1,2,0:T(8,128)(2,1)S(1)}, u32[]{:S(2)}, u32[]{:S(2)}) %collective-permute-start.3) | collective-permute-done | bytes 1048608 | tf_op jit(solution)/shard_map/ppermute | solution.py:14
  121.6 5.2 %fusion.51 = bf16[2,256,1024]{2,1,0:T(8,128)(2,1)S(1)} fusion(bf16[2,256,2048]{2,1,0:T(8,128)(2,1)} %all-gather.2.cloned.1.call-done, bf16[1024,2048]{1,0:T(8,128)(2,1)} %param.11), kind=kOutput, calls=%fused_computation.65 | convolution fusion | flops 2148007936 | bytes 7340032 | tf_op jit(solution)/shard_map/brf,df->brd/dot_general | solution.py:87
  129.7 115.5 %while.20 = (s32[]{:T(128)}, bf16[8,2,256,128]{2,3,0,1:T(8,128)(2,1)}, bf16[8,2,256,128]{3,2,1,0:T(8,128)(2,1)}, f32[8,2,256,128]{3,2,1,0:T(8,128)}, f32[8,2,256...) while((s32[]{:T(128)}, ...), condition=%wide.region_4.5_spmd, body=%wide.region_0.4_spmd.sunk | while | flops 1422130176 | bytes 37054616 | solution.py:112
  146.9 2.7 bitcast_dynamic-update-slice_fusion.2
  245.2 6.8 %fusion.35 = f32[2,256,2048]{2,1,0:T(8,128)} fusion(bf16[2,256,1024]{1,2,0:T(8,128)(2,1)} %bitcast.233, bf16[1024,2048]{1,0:T(8,128)(2,1)} %param.11), kind=kOutput, calls=%fused_computation.47 | convolution fusion | flops 2147483648 | bytes 9437184 | tf_op jit(solution)/shard_map/brd,df->brf/dot_general | solution.py:126
  252.0 5.4 %slice_bitcast_fusion.7 = (bf16[8,2,32,8,128]{4,3,2,1,0:T(8,128)(2,1)S(1)}, bf16[8,2,32,8,128]{4,3,2,1,0:T(8,128)(2,1)S(1)}, bf16[8,2,32,8,128]{4,3,2,1,0:T(8,12...) fusion(bf16[8,2,1536,128]{3,2,1,0:T(8,128)(2,1)} %get-tuple-ele, ...), kind=kLoop, calls=%fused_computation.84 | loop fusion | bytes 25165824
  262.0 7.0 %collective-permute-start.16 = (bf16[2,256,1024]{2,1,0:T(8,128)(2,1)S(1)}, bf16[2,256,1024]{2,1,0:T(8,128)(2,1)S(1)}, u32[]{:S(2)}, u32[]{:S(2)}) collective-permute-start(bf16[2,256,1024]{2,1,0:T(8,128)(2,1)S(1)} %bitcast.243), channel_id=1, source_target_pairs={{32,0},{34,2},{36,4},{38,6},{40,8},{42,10},{44,12},{46,14},{48,16}... | collective-permute-start | bytes 3145736 | tf_op jit(solution)/shard_map/ppermute | solution.py:14
  269.0 5.9 %collective-permute-start.15 = (bf16[2,256,1024]{2,1,0:T(8,128)(2,1)S(1)}, bf16[2,256,1024]{2,1,0:T(8,128)(2,1)S(1)}, u32[]{:S(2)}, u32[]{:S(2)}) collective-permute-start(bf16[2,256,1024]{2,1,0:T(8,128)(2,1)S(1)} %bitcast.240), channel_id=1, source_target_pairs={{16,0},{18,2},{20,4},{22,6},{24,8},{26,10},{28,12},{30,14},{48,32}... | collective-permute-start | bytes 3145736 | tf_op jit(solution)/shard_map/ppermute | solution.py:14
  277.8 10.8 %collective-permute-done.17 = bf16[2,256,1024]{2,1,0:T(8,128)(2,1)S(1)} collective-permute-done((bf16[2,256,1024]{2,1,0:T(8,128)(2,1)S(1)}, bf16[2,256,1024]{2,1,0:T(8,128)(2,1)S(1)}, u32[]{:S(2)}, u32[]{:S(2)}) %collective-permute-start.17) | collective-permute-done | bytes 1048608 | tf_op jit(solution)/shard_map/ppermute | solution.py:14
  293.5 4.8 %collective-permute-done.15 = bf16[2,256,1024]{2,1,0:T(8,128)(2,1)S(1)} collective-permute-done((bf16[2,256,1024]{2,1,0:T(8,128)(2,1)S(1)}, bf16[2,256,1024]{2,1,0:T(8,128)(2,1)S(1)}, u32[]{:S(2)}, u32[]{:S(2)}) %collective-permute-start.15) | collective-permute-done | bytes 1048608 | tf_op jit(solution)/shard_map/ppermute | solution.py:14
  298.3 5.9 %collective-permute-start.21 = (bf16[2,256,1024]{2,1,0:T(8,128)(2,1)S(1)}, bf16[2,256,1024]{2,1,0:T(8,128)(2,1)S(1)}, u32[]{:S(2)}, u32[]{:S(2)}) collective-permute-start(bf16[2,256,1024]{2,1,0:T(8,128)(2,1)S(1)} %bitcast.239), channel_id=1, source_target_pairs={{16,0},{18,2},{20,4},{22,6},{24,8},{26,10},{28,12},{30,14},{48,32}... | collective-permute-start | bytes 3145736 | tf_op jit(solution)/shard_map/ppermute | solution.py:14
  304.2 16.6 %collective-permute-done.14 = bf16[2,256,1024]{2,1,0:T(8,128)(2,1)S(1)} collective-permute-done((bf16[2,256,1024]{2,1,0:T(8,128)(2,1)S(1)}, bf16[2,256,1024]{2,1,0:T(8,128)(2,1)S(1)}, u32[]{:S(2)}, u32[]{:S(2)}) %collective-permute-start.14) | collective-permute-done | bytes 1048608 | tf_op jit(solution)/shard_map/ppermute | solution.py:14
  322.2 6.1 %collective-permute-done.13 = bf16[2,256,1024]{2,1,0:T(8,128)(2,1)S(1)} collective-permute-done((bf16[2,256,1024]{2,1,0:T(8,128)(2,1)S(1)}, bf16[2,256,1024]{2,1,0:T(8,128)(2,1)S(1)}, u32[]{:S(2)}, u32[]{:S(2)}) %collective-permute-start.13) | collective-permute-done | bytes 1048608 | tf_op jit(solution)/shard_map/ppermute | solution.py:14
  329.6 29.6 %collective-permute-done.19 = bf16[2,256,1024]{2,1,0:T(8,128)(2,1)S(1)} collective-permute-done((bf16[2,256,1024]{2,1,0:T(8,128)(2,1)S(1)}, bf16[2,256,1024]{2,1,0:T(8,128)(2,1)S(1)}, u32[]{:S(2)}, u32[]{:S(2)}) %collective-permute-start.19) | collective-permute-done | bytes 1048608 | tf_op jit(solution)/shard_map/ppermute | solution.py:14
  364.2 7.0 %collective-permute-done.23 = bf16[2,256,1024]{2,1,0:T(8,128)(2,1)S(1)} collective-permute-done((bf16[2,256,1024]{2,1,0:T(8,128)(2,1)S(1)}, bf16[2,256,1024]{2,1,0:T(8,128)(2,1)S(1)}, u32[]{:S(2)}, u32[]{:S(2)}) %collective-permute-start.23) | collective-permute-done | bytes 1048608 | tf_op jit(solution)/shard_map/ppermute | solution.py:14
  373.8 2.7 convert_element_type.69
  (180 shorter events, 173.8 us)
Async XLA Ops:
  7.2 114.4 %all-gather.2.cloned.1.call-start = ((), (), s32[]{:S(2)}) async-start(), calls=%async_computation.1 | async-start | bytes 3145728 | tf_op jit(solution)/shard_map/all_gather | solution.py:89
  8.8 26.6 %collective-permute-start.11 = (bf16[2,256,1024]{1,2,0:T(8,128)(2,1)S(1)}, bf16[2,256,1024]{1,2,0:T(8,128)(2,1)}, u32[]{:S(2)}, u32[]{:S(2)}) collective-permute-start(bf16[2,256,1024]{1,2,0:T(8,128)(2,1)S(1)} %copy.50), channel_id=1, source_target_pairs={{0,64},{2,66},{4,68},{6,70},{8,72},{10,74},{12,76},{14,78},{16,80}... | collective-permute-start | bytes 3145736 | tf_op jit(solution)/shard_map/ppermute | solution.py:14
  14.0 45.8 %collective-permute-start.10 = (bf16[2,256,1024]{1,2,0:T(8,128)(2,1)S(1)}, bf16[2,256,1024]{1,2,0:T(8,128)(2,1)}, u32[]{:S(2)}, u32[]{:S(2)}) collective-permute-start(bf16[2,256,1024]{1,2,0:T(8,128)(2,1)S(1)} %copy.50), channel_id=1, source_target_pairs={{0,32},{2,34},{4,36},{6,38},{8,40},{10,42},{12,44},{14,46},{16,48}... | collective-permute-start | bytes 3145736 | tf_op jit(solution)/shard_map/ppermute | solution.py:14
  15.3 51.0 %collective-permute-start.9 = (bf16[2,256,1024]{1,2,0:T(8,128)(2,1)S(1)}, bf16[2,256,1024]{1,2,0:T(8,128)(2,1)}, u32[]{:S(2)}, u32[]{:S(2)}) collective-permute-start(bf16[2,256,1024]{1,2,0:T(8,128)(2,1)S(1)} %copy.50), channel_id=1, source_target_pairs={{0,16},{2,18},{4,20},{6,22},{8,24},{10,26},{12,28},{14,30},{32,48}... | collective-permute-start | bytes 3145736 | tf_op jit(solution)/shard_map/ppermute | solution.py:14
  16.6 59.6 %collective-permute-start.7 = (bf16[2,256,1024]{1,2,0:T(8,128)(2,1)S(1)}, bf16[2,256,1024]{1,2,0:T(8,128)(2,1)}, u32[]{:S(2)}, u32[]{:S(2)}) collective-permute-start(bf16[2,256,1024]{1,2,0:T(8,128)(2,1)S(1)} %copy.50), channel_id=1, source_target_pairs={{0,4},{2,6},{8,12},{10,14},{16,20},{18,22},{24,28},{26,30},{32,36}... | collective-permute-start | bytes 3145736 | tf_op jit(solution)/shard_map/ppermute | solution.py:14
  22.5 48.8 %collective-permute-start.6 = (bf16[2,256,1024]{1,2,0:T(8,128)(2,1)S(1)}, bf16[2,256,1024]{1,2,0:T(8,128)(2,1)}, u32[]{:S(2)}, u32[]{:S(2)}) collective-permute-start(bf16[2,256,1024]{1,2,0:T(8,128)(2,1)S(1)} %copy.50), channel_id=1, source_target_pairs={{0,2},{4,6},{8,10},{12,14},{16,18},{20,22},{24,26},{28,30},{32,34}... | collective-permute-start | bytes 3145736 | tf_op jit(solution)/shard_map/ppermute | solution.py:14
  24.8 349.0 %reduce-scatter.2.cloned.1.call-start = ((), (), s32[]{:S(2)}) async-start(), calls=%async_computation.2 | async-start | bytes 6291456 | tf_op jit(solution)/shard_map/reduce_scatter | solution.py:127
  35.4 43.4 %collective-permute-start.8 = (bf16[2,256,1024]{1,2,0:T(8,128)(2,1)S(1)}, bf16[2,256,1024]{1,2,0:T(8,128)(2,1)}, u32[]{:S(2)}, u32[]{:S(2)}) collective-permute-start(bf16[2,256,1024]{1,2,0:T(8,128)(2,1)S(1)} %copy.50), channel_id=1, source_target_pairs={{0,8},{2,10},{4,12},{6,14},{16,24},{18,26},{20,28},{22,30},{32,40}... | collective-permute-start | bytes 3145736 | tf_op jit(solution)/shard_map/ppermute | solution.py:14
  59.8 21.6 %collective-permute-start = (bf16[2,256,1024]{1,2,0:T(8,128)(2,1)}, bf16[2,256,1024]{1,2,0:T(8,128)(2,1)}, u32[]{:S(2)}, u32[]{:S(2)}) collective-permute-start(bf16[2,256,1024]{1,2,0:T(8,128)(2,1)} %copy.43), channel_id=1, source_target_pairs={{0,2},{4,6},{8,10},{12,14},{16,18},{20,22},{24,26},{28,30},{32,34}... | collective-permute-start | bytes 3145736 | tf_op jit(solution)/shard_map/ppermute | solution.py:14
  66.2 25.8 %collective-permute-start.1 = (bf16[2,256,1024]{1,2,0:T(8,128)(2,1)}, bf16[2,256,1024]{1,2,0:T(8,128)(2,1)S(1)}, u32[]{:S(2)}, u32[]{:S(2)}) collective-permute-start(bf16[2,256,1024]{1,2,0:T(8,128)(2,1)} %copy.43), channel_id=1, source_target_pairs={{0,4},{2,6},{8,12},{10,14},{16,20},{18,22},{24,28},{26,30},{32,36}... | collective-permute-start | bytes 3145736 | tf_op jit(solution)/shard_map/ppermute | solution.py:14
  71.3 24.1 %collective-permute-start.2 = (bf16[2,256,1024]{1,2,0:T(8,128)(2,1)}, bf16[2,256,1024]{1,2,0:T(8,128)(2,1)S(1)}, u32[]{:S(2)}, u32[]{:S(2)}) collective-permute-start(bf16[2,256,1024]{1,2,0:T(8,128)(2,1)} %copy.43), channel_id=1, source_target_pairs={{0,8},{2,10},{4,12},{6,14},{16,24},{18,26},{20,28},{22,30},{32,40}... | collective-permute-start | bytes 3145736 | tf_op jit(solution)/shard_map/ppermute | solution.py:14
  76.2 42.0 %collective-permute-start.3 = (bf16[2,256,1024]{1,2,0:T(8,128)(2,1)}, bf16[2,256,1024]{1,2,0:T(8,128)(2,1)S(1)}, u32[]{:S(2)}, u32[]{:S(2)}) collective-permute-start(bf16[2,256,1024]{1,2,0:T(8,128)(2,1)} %copy.43), channel_id=1, source_target_pairs={{0,16},{2,18},{4,20},{6,22},{8,24},{10,26},{12,28},{14,30},{32,48}... | collective-permute-start | bytes 3145736 | tf_op jit(solution)/shard_map/ppermute | solution.py:14
  78.8 40.5 %collective-permute-start.4 = (bf16[2,256,1024]{1,2,0:T(8,128)(2,1)}, bf16[2,256,1024]{1,2,0:T(8,128)(2,1)S(1)}, u32[]{:S(2)}, u32[]{:S(2)}) collective-permute-start(bf16[2,256,1024]{1,2,0:T(8,128)(2,1)} %copy.43), channel_id=1, source_target_pairs={{0,32},{2,34},{4,36},{6,38},{8,40},{10,42},{12,44},{14,46},{16,48}... | collective-permute-start | bytes 3145736 | tf_op jit(solution)/shard_map/ppermute | solution.py:14
  81.4 39.1 %collective-permute-start.5 = (bf16[2,256,1024]{1,2,0:T(8,128)(2,1)}, bf16[2,256,1024]{1,2,0:T(8,128)(2,1)S(1)}, u32[]{:S(2)}, u32[]{:S(2)}) collective-permute-start(bf16[2,256,1024]{1,2,0:T(8,128)(2,1)} %copy.43), channel_id=1, source_target_pairs={{0,64},{2,66},{4,68},{6,70},{8,72},{10,74},{12,76},{14,78},{16,80}... | collective-permute-start | bytes 3145736 | tf_op jit(solution)/shard_map/ppermute | solution.py:14
  259.3 29.2 %collective-permute-start.17 = (bf16[2,256,1024]{2,1,0:T(8,128)(2,1)S(1)}, bf16[2,256,1024]{2,1,0:T(8,128)(2,1)S(1)}, u32[]{:S(2)}, u32[]{:S(2)}) collective-permute-start(bf16[2,256,1024]{2,1,0:T(8,128)(2,1)S(1)} %bitcast.244), channel_id=1, source_target_pairs={{64,0},{66,2},{68,4},{70,6},{72,8},{74,10},{76,12},{78,14},{80,16}... | collective-permute-start | bytes 3145736 | tf_op jit(solution)/shard_map/ppermute | solution.py:14
  262.0 30.2 %collective-permute-start.16 = (bf16[2,256,1024]{2,1,0:T(8,128)(2,1)S(1)}, bf16[2,256,1024]{2,1,0:T(8,128)(2,1)S(1)}, u32[]{:S(2)}, u32[]{:S(2)}) collective-permute-start(bf16[2,256,1024]{2,1,0:T(8,128)(2,1)S(1)} %bitcast.243), channel_id=1, source_target_pairs={{32,0},{34,2},{36,4},{38,6},{40,8},{42,10},{44,12},{46,14},{48,16}... | collective-permute-start | bytes 3145736 | tf_op jit(solution)/shard_map/ppermute | solution.py:14
  269.0 29.3 %collective-permute-start.15 = (bf16[2,256,1024]{2,1,0:T(8,128)(2,1)S(1)}, bf16[2,256,1024]{2,1,0:T(8,128)(2,1)S(1)}, u32[]{:S(2)}, u32[]{:S(2)}) collective-permute-start(bf16[2,256,1024]{2,1,0:T(8,128)(2,1)S(1)} %bitcast.240), channel_id=1, source_target_pairs={{16,0},{18,2},{20,4},{22,6},{24,8},{26,10},{28,12},{30,14},{48,32}... | collective-permute-start | bytes 3145736 | tf_op jit(solution)/shard_map/ppermute | solution.py:14
  275.2 45.7 %collective-permute-start.14 = (bf16[2,256,1024]{2,1,0:T(8,128)(2,1)S(1)}, bf16[2,256,1024]{2,1,0:T(8,128)(2,1)S(1)}, u32[]{:S(2)}, u32[]{:S(2)}) collective-permute-start(bf16[2,256,1024]{2,1,0:T(8,128)(2,1)S(1)} %bitcast.242), channel_id=1, source_target_pairs={{8,0},{10,2},{12,4},{14,6},{24,16},{26,18},{28,20},{30,22},{40,32}... | collective-permute-start | bytes 3145736 | tf_op jit(solution)/shard_map/ppermute | solution.py:14
  276.5 51.9 %collective-permute-start.13 = (bf16[2,256,1024]{2,1,0:T(8,128)(2,1)S(1)}, bf16[2,256,1024]{2,1,0:T(8,128)(2,1)S(1)}, u32[]{:S(2)}, u32[]{:S(2)}) collective-permute-start(bf16[2,256,1024]{2,1,0:T(8,128)(2,1)S(1)} %bitcast.236), channel_id=1, source_target_pairs={{4,0},{6,2},{12,8},{14,10},{20,16},{22,18},{28,24},{30,26},{36,32}... | collective-permute-start | bytes 3145736 | tf_op jit(solution)/shard_map/ppermute | solution.py:14
  288.5 70.7 %collective-permute-start.19 = (bf16[2,256,1024]{2,1,0:T(8,128)(2,1)S(1)}, bf16[2,256,1024]{2,1,0:T(8,128)(2,1)S(1)}, u32[]{:S(2)}, u32[]{:S(2)}) collective-permute-start(bf16[2,256,1024]{2,1,0:T(8,128)(2,1)S(1)} %bitcast.234), channel_id=1, source_target_pairs={{4,0},{6,2},{12,8},{14,10},{20,16},{22,18},{28,24},{30,26},{36,32}... | collective-permute-start | bytes 3145736 | tf_op jit(solution)/shard_map/ppermute | solution.py:14
  292.2 72.0 %collective-permute-start.20 = (bf16[2,256,1024]{2,1,0:T(8,128)(2,1)S(1)}, bf16[2,256,1024]{2,1,0:T(8,128)(2,1)S(1)}, u32[]{:S(2)}, u32[]{:S(2)}) collective-permute-start(bf16[2,256,1024]{2,1,0:T(8,128)(2,1)S(1)} %bitcast.241), channel_id=1, source_target_pairs={{8,0},{10,2},{12,4},{14,6},{24,16},{26,18},{28,20},{30,22},{40,32}... | collective-permute-start | bytes 3145736 | tf_op jit(solution)/shard_map/ppermute | solution.py:14
  298.3 65.9 %collective-permute-start.21 = (bf16[2,256,1024]{2,1,0:T(8,128)(2,1)S(1)}, bf16[2,256,1024]{2,1,0:T(8,128)(2,1)S(1)}, u32[]{:S(2)}, u32[]{:S(2)}) collective-permute-start(bf16[2,256,1024]{2,1,0:T(8,128)(2,1)S(1)} %bitcast.239), channel_id=1, source_target_pairs={{16,0},{18,2},{20,4},{22,6},{24,8},{26,10},{28,12},{30,14},{48,32}... | collective-permute-start | bytes 3145736 | tf_op jit(solution)/shard_map/ppermute | solution.py:14
  320.9 43.4 %collective-permute-start.22 = (bf16[2,256,1024]{2,1,0:T(8,128)(2,1)S(1)}, bf16[2,256,1024]{2,1,0:T(8,128)(2,1)S(1)}, u32[]{:S(2)}, u32[]{:S(2)}) collective-permute-start(bf16[2,256,1024]{2,1,0:T(8,128)(2,1)S(1)} %bitcast.238), channel_id=1, source_target_pairs={{32,0},{34,2},{36,4},{38,6},{40,8},{42,10},{44,12},{46,14},{48,16}... | collective-permute-start | bytes 3145736 | tf_op jit(solution)/shard_map/ppermute | solution.py:14
  328.4 42.9 %collective-permute-start.23 = (bf16[2,256,1024]{2,1,0:T(8,128)(2,1)S(1)}, bf16[2,256,1024]{2,1,0:T(8,128)(2,1)S(1)}, u32[]{:S(2)}, u32[]{:S(2)}) collective-permute-start(bf16[2,256,1024]{2,1,0:T(8,128)(2,1)S(1)} %bitcast.237), channel_id=1, source_target_pairs={{64,0},{66,2},{68,4},{70,6},{72,8},{74,10},{76,12},{78,14},{80,16}... | collective-permute-start | bytes 3145736 | tf_op jit(solution)/shard_map/ppermute | solution.py:14
  (7 other events, 246.6 us)
Sparse Core Ops, SparseCore 0:
  24.9 42.4 all-gather.1
  252.2 61.9 reduce-scatter.1

commit v2 on v1

v2 whole, which is shorter than its diff:
```python
import functools
import math

import jax
import jax.numpy as jnp
from jax import lax
from jax.experimental import pallas as pl
from jax.experimental.pallas import tpu as pltpu
from jax.sharding import PartitionSpec as P

HEAD_DIM = 128
GROUP = 2
MESH = pl.DeviceIdType.MESH
F32 = jnp.float32
BF16 = jnp.bfloat16
LOW = -1e30
TILE = 32


def dot_nt(a, b):
    return lax.dot_general(a, b, (((1,), (1,)), ((), ())), preferred_element_type=F32)


def dot_nn(a, b):
    return lax.dot_general(a, b, (((1,), (0,)), ((), ())), preferred_element_type=F32)


def dot_tn(a, b):
    return lax.dot_general(a, b, (((0,), (0,)), ((), ())), preferred_element_type=F32)


def kernel(
    levels, q_in, k_in, v_in, og_in, w_in, lo_out, dq_out, dk_out, dv_out,
    q, kv, far, do, w, og, og_far, attn, s, p, dp, ds, top, norm, acc, own, dq, po, po_far, lo,
    ld_q, ld_kv, ld_og, ld_w, og_send, og_recv, po_send, po_recv, kv_send, kv_recv, out_sem, grad_sem,
):
    me = lax.axis_index("seq")
    hd = lax.axis_index("head")
    chunks, rows, width = q.shape
    batch = og.shape[0]
    half = og.shape[2]
    per = chunks // batch
    scale = HEAD_DIM ** -0.5
    rate = scale * math.log2(math.e)
    own_cols = pl.multiple_of(hd * half, half)
    far_cols = pl.multiple_of((1 - hd) * half, half)

    def bit(j):
        return lax.rem(lax.shift_right_logical(me, j), 2)

    def partner(j):
        return me + (1 - 2 * bit(j)) * (1 << j)

    def cols(c):
        return pl.ds(pl.multiple_of(lax.rem(c, per) * width, width), width)

    def load_kv(c, i):
        src = (k_in, v_in)[i].at[lax.div(c, per), :, cols(c)]
        return pltpu.make_async_copy(src, kv.at[c, i], ld_kv.at[c, i])

    def load_q(c):
        return pltpu.make_async_copy(q_in.at[lax.div(c, per), :, cols(c)], q.at[c], ld_q.at[c])

    def load_og(b):
        return pltpu.make_async_copy(og_in.at[b], og.at[b], ld_og.at[b])

    load_w = pltpu.make_async_copy(w_in, w, ld_w)

    def send_og(b):
        return pltpu.make_async_remote_copy(
            og_in.at[b], og_far.at[b], og_send.at[b], og_recv.at[b],
            device_id=(me, 1 - hd), device_id_type=MESH)

    def send_po(b):
        return pltpu.make_async_remote_copy(
            po.at[b], po_far.at[b], po_send.at[b], po_recv.at[b],
            device_id=(me, 1 - hd), device_id_type=MESH)

    def send_kv(j, c):
        return pltpu.make_async_remote_copy(
            kv.at[c], far.at[j, c], kv_send.at[j, c], kv_recv.at[j, c],
            device_id=(partner(j), hd), device_id_type=MESH)

    def send_grad(j, c):
        return pltpu.make_async_remote_copy(
            far.at[j, c], far.at[j, c], kv_send.at[j, c], kv_recv.at[j, c],
            device_id=(partner(j), hd), device_id_type=MESH)

    def put_dq(c):
        return pltpu.make_async_copy(dq.at[c], dq_out.at[lax.div(c, per), :, cols(c)], out_sem.at[c])

    def put_grad(c, i):
        dst = (dk_out, dv_out)[i].at[lax.div(c, per), :, cols(c)]
        return pltpu.make_async_copy(kv.at[c, i], dst, grad_sem.at[c, i])

    def start_loads(c, carry):
        load_kv(c, 0).start()
        load_kv(c, 1).start()
        return carry

    lax.fori_loop(0, chunks, start_loads, 0)
    for b in range(batch):
        load_og(b).start()

    def start_q(c, carry):
        load_q(c).start()
        return carry

    lax.fori_loop(0, chunks, start_q, 0)
    load_w.start()

    barrier = pltpu.get_barrier_semaphore()
    for j in range(levels):
        pl.semaphore_signal(barrier, inc=1, device_id=(partner(j), hd), device_id_type=MESH)
    pl.semaphore_signal(barrier, inc=1, device_id=(me, 1 - hd), device_id_type=MESH)
    pl.semaphore_wait(barrier, levels + 1)

    send_og(0).start()

    def start_sends(c, carry):
        load_kv(c, 0).wait()
        load_kv(c, 1).wait()
        for j in range(levels):
            @pl.when(bit(j) == 0)
            def _():
                send_kv(j, c).start()

        if batch > 1:
            @pl.when(c == 1)
            def _():
                for b in range(1, batch):
                    send_og(b).start()
        return carry

    lax.fori_loop(0, chunks, start_sends, 0)
    for b in range(batch):
        load_og(b).wait()
    lax.fori_loop(0, chunks, lambda c, carry: (load_q(c).wait(), carry)[1], 0)
    load_w.wait()

    heads = [slice(u * HEAD_DIM, (u + 1) * HEAD_DIM) for u in range(GROUP)]
    tiles = [slice(t, t + TILE) for t in range(0, rows, TILE)]

    def absorb(slot, u):
        peak = s[slot, u, tiles[0], :]
        for t in tiles[1:]:
            peak = jnp.maximum(peak, s[slot, u, t, :])
        old = top[u]
        new = jnp.maximum(old, jnp.max(peak, axis=0, keepdims=True))
        total = None
        for t in tiles:
            e = jnp.exp2((s[slot, u, t, :] - new) * rate)
            total = e if total is None else total + e
        norm[u] = norm[u] * jnp.exp2((old - new) * rate) + jnp.sum(total, axis=0, keepdims=True)
        top[u] = new

    def weigh(slot, u, value_ref):
        shift = norm[u]
        for t in tiles:
            e = jnp.exp2(s[slot, u, t, :] * rate - shift)
            s[slot, u, t, :] = e
            p[slot, u, t, :] = e.astype(BF16)
        acc[u] += dot_tn(value_ref[:, heads[u]], p[slot, u])

    def back(slot, u, c, key_ref, value_ref):
        dsum = norm[u]
        dp[u] = dot_nt(value_ref[:, heads[u]], do[c, :, heads[u]])
        for t in tiles:
            ds[u, t, :] = (s[slot, u, t, :] * (dp[u, t, :] - dsum)).astype(BF16)
        acc[u] += dot_tn(key_ref[:, heads[u]], ds[u])
        key_term = dot_nn(ds[u], q[c, :, heads[u]]) * scale
        value_term = dot_nn(p[slot, u], do[c, :, heads[u]])
        return key_term, value_term

    def per_chunk(c, carry):
        b = lax.div(c, per)
        for u in range(GROUP):
            top[u] = jnp.full((1, rows), LOW, F32)
            norm[u] = jnp.zeros((1, rows), F32)
            scores = dot_nt(kv[c, 0, :, heads[u]], q[c, :, heads[u]])
            s[levels, u] = scores
        for u in range(GROUP):
            for t in tiles:
                at = lax.broadcasted_iota(jnp.int32, (TILE, rows), 0) + t.start
                to = lax.broadcasted_iota(jnp.int32, (TILE, rows), 1)
                s[levels, u, t, :] = jnp.where(at <= to, s[levels, u, t, :], LOW)
            absorb(levels, u)

        def score(j, carry):
            @pl.when(bit(j) == 1)
            def _():
                send_kv(j, c).wait_recv()
                for u in range(GROUP):
                    s[j, u] = dot_nt(far[j, c, 0, :, heads[u]], q[c, :, heads[u]])
                for u in range(GROUP):
                    absorb(j, u)
            return carry

        lax.fori_loop(0, levels, score, 0)

        @pl.when(lax.rem(c, per) == 0)
        def _():
            send_og(b).wait_recv()
        w_rows = pl.ds(pl.multiple_of(lax.rem(c, per) * width, width), width)
        do[c] = (
            dot_nt(og[b], w[w_rows, pl.ds(own_cols, half)])
            + dot_nt(og_far[b], w[w_rows, pl.ds(far_cols, half)])
        ).astype(BF16)

        for u in range(GROUP):
            norm[u] = top[u] * rate + jnp.log2(norm[u])
            acc[u] = jnp.zeros((HEAD_DIM, rows), F32)
        for u in range(GROUP):
            weigh(levels, u, kv.at[c, 1])

        def weighted(j, carry):
            @pl.when(bit(j) == 1)
            def _():
                for u in range(GROUP):
                    weigh(j, u, far.at[j, c, 1])
            return carry

        lax.fori_loop(0, levels, weighted, 0)

        for u in range(GROUP):
            mixed = acc[u].astype(BF16).astype(F32)
            lean = do[c, :, heads[u]].astype(F32).T
            norm[u] = jnp.sum(mixed * lean, axis=0, keepdims=True)
            at = pl.multiple_of(lax.rem(c, per) * width, width) + u * HEAD_DIM
            attn[b, :, pl.ds(pl.multiple_of(at, HEAD_DIM), HEAD_DIM)] = mixed.T.astype(BF16)
            acc[u] = jnp.zeros((HEAD_DIM, rows), F32)

        @pl.when(lax.rem(c, per) == per - 1)
        def _():
            for t in range(0, half, width):
                at = pl.ds(pl.multiple_of(far_cols + t, width), width)
                po[b, :, t:t + width] = dot_nn(attn[b], w[:, at]).astype(BF16)
            send_po(b).start()
            for t in range(0, half, width):
                at = pl.ds(pl.multiple_of(own_cols + t, width), width)
                lo[b, :, t:t + width] = dot_nn(attn[b], w[:, at])

        for u in range(GROUP):
            key_term, value_term = back(levels, u, c, kv.at[c, 0], kv.at[c, 1])
            own[c, 0, :, heads[u]] = key_term
            own[c, 1, :, heads[u]] = value_term

        def backward(j, carry):
            @pl.when(bit(j) == 1)
            def _():
                for u in range(GROUP):
                    key_term, value_term = back(j, u, c, far.at[j, c, 0], far.at[j, c, 1])
                    far[j, c, 0, :, heads[u]] = key_term.astype(BF16)
                    far[j, c, 1, :, heads[u]] = value_term.astype(BF16)
            return carry

        lax.fori_loop(0, levels, backward, 0)
        for u in range(GROUP):
            dq[c, :, heads[u]] = (acc[u] * scale).T.astype(BF16)
        put_dq(c).start()
        for j in range(levels):
            @pl.when(bit(j) == 1)
            def _():
                send_grad(j, c).start()
        return carry

    lax.fori_loop(0, chunks, per_chunk, 0)

    def finish(c, carry):
        for j in range(levels):
            @pl.when(bit(j) == 0)
            def _():
                send_kv(j, c).wait_send()
                send_grad(j, c).wait_recv()
                for i in range(2):
                    for t in tiles:
                        own[c, i, t, :] += far[j, c, i, t, :].astype(F32)
        for i in range(2):
            for t in tiles:
                kv[c, i, t, :] = own[c, i, t, :].astype(BF16)
            put_grad(c, i).start()
        return carry

    lax.fori_loop(0, chunks, finish, 0)

    outs = []
    for b in range(batch):
        send_po(b).wait_recv()
        send_og(b).wait_send()
        for t in tiles:
            og[b, t, :] = (lo[b, t, :] + po_far[b, t, :].astype(F32)).astype(BF16)
        copy = pltpu.make_async_copy(og.at[b], lo_out.at[b], ld_og.at[b])
        copy.start()
        outs.append(copy)

    def drain(c, carry):
        put_dq(c).wait()
        put_grad(c, 0).wait()
        put_grad(c, 1).wait()
        for j in range(levels):
            @pl.when(bit(j) == 1)
            def _():
                send_grad(j, c).wait_send()
        return carry

    lax.fori_loop(0, chunks, drain, 0)
    for b in range(batch):
        send_po(b).wait_send()
        outs[b].wait()


def solution(mesh):
    levels = mesh.shape["seq"].bit_length() - 1

    def step(queries, key_states, value_states, output_grad, out_proj):
        batch, rows, half = queries.shape
        width = GROUP * HEAD_DIM
        chunks = batch * (half // width)
        shape = jax.ShapeDtypeStruct(queries.shape, BF16)
        hbm = pl.BlockSpec(memory_space=pl.ANY)
        dma = pltpu.SemaphoreType.DMA
        return tuple(pl.pallas_call(
            functools.partial(kernel, levels),
            name="butterfly",
            out_shape=[shape] * 4,
            in_specs=[hbm] * 5,
            out_specs=[hbm] * 4,
            scratch_shapes=[
                pltpu.VMEM((chunks, rows, width), BF16),
                pltpu.VMEM((chunks, 2, rows, width), BF16),
                pltpu.VMEM((levels, chunks, 2, rows, width), BF16),
                pltpu.VMEM((chunks, rows, width), BF16),
                pltpu.VMEM(out_proj.shape, BF16),
                pltpu.VMEM((batch, rows, half), BF16),
                pltpu.VMEM((batch, rows, half), BF16),
                pltpu.VMEM((batch, rows, half), BF16),
                pltpu.VMEM((levels + 1, GROUP, rows, rows), F32),
                pltpu.VMEM((levels + 1, GROUP, rows, rows), BF16),
                pltpu.VMEM((GROUP, rows, rows), F32),
                pltpu.VMEM((GROUP, rows, rows), BF16),
                pltpu.VMEM((GROUP, 1, rows), F32),
                pltpu.VMEM((GROUP, 1, rows), F32),
                pltpu.VMEM((GROUP, HEAD_DIM, rows), F32),
                pltpu.VMEM((chunks, 2, rows, width), F32),
                pltpu.VMEM((chunks, rows, width), BF16),
                pltpu.VMEM((batch, rows, half), BF16),
                pltpu.VMEM((batch, rows, half), BF16),
                pltpu.VMEM((batch, rows, half), F32),
                dma((chunks,)),
                dma((chunks, 2)),
                dma((batch,)),
                dma,
                dma((batch,)),
                dma((batch,)),
                dma((batch,)),
                dma((batch,)),
                dma((levels, chunks)),
                dma((levels, chunks)),
                dma((chunks,)),
                dma((chunks, 2)),
            ],
            compiler_params=pltpu.CompilerParams(
                collective_id=0, has_side_effects=True, vmem_limit_bytes=60 << 20
            ),
        )(queries, key_states, value_states, output_grad, out_proj))

    act = P(None, "seq", "head")
    return jax.shard_map(
        step, mesh=mesh, in_specs=(act, act, act, act, P("head", None)),
        out_specs=(act,) * 4, check_vma=False,
    )
```

time: 386 us -> 133 us (0.34)
  the two profiles are of different devices: /device:TPU:72 before, /device:TPU:14 now
where the time goes in v2:
time: 133 us; the launch traced here: 132 us
  Pallas kernels  124 us (93%)
  local copies, waits for them, and re-layouts  6.62 us (5%)
    pallas_call x1, Pallas kernels, step(): pl.pallas_call(functools.partial(kernel, levels), name='butterfly', out_s...  124 us
    unnamed x8, local copies, waits for them, and re-layouts  6.62 us

profile of v2, /device:TPU:14, one launch (start us, length us, event | category | flops | bytes accessed | tf_op | source)
XLA Modules:
  0.0 131.5 jit_solution(17573798337051519244)
XLA Ops:
  0.6 124.2 %butterfly.1 = (bf16[2,256,1024]{2,1,0:T(8,128)(2,1)}, bf16[2,256,1024]{2,1,0:T(8,128)(2,1)}, bf16[2,256,1024]{2,1,0:T(8,128)(2,1)}, bf16[2,256,1024]{2,1,0:T(8,128)(2,1)}) custom-call(bf16[2,256,1024]{2,1,0:T(8,128)(2,1)} %q_in.1, bf16[2,256,1024]{2,1,0:T(8,128)(2,1)} %k_in.1, bf16[2,256,1024]{2,1,0:T(8,128)(2,1)} %v_in.1, bf16[2,256,1024]{2,1,0:T(8,128)(2,1)} %og_in.1, ...), custom_call_target="tpu_custom_call" | custom-call | tf_op jit(solution)/shard_map/butterfly/pallas_call | solution.py:322
  124.9 0.0 copy-start.1
  124.9 0.0 copy-start
  124.9 2.4 %copy.13 = bf16[2,256,1024]{2,1,0:T(8,128)(2,1)} copy(bf16[2,256,1024]{2,1,0:T(8,128)(2,1)} %get-tuple-element.8) | data formatting | bytes 2097152
  127.3 2.3 %copy.14 = bf16[2,256,1024]{2,1,0:T(8,128)(2,1)} copy(bf16[2,256,1024]{2,1,0:T(8,128)(2,1)} %get-tuple-element.9) | data formatting | bytes 2097152
  129.6 0.0 copy-done.1
  129.6 1.0 copy.15
  130.6 0.0 copy-done
  130.6 1.0 copy.16
Async XLA Ops:
  124.9 4.7 %copy-start.1 = (bf16[2,256,1024]{2,1,0:T(8,128)(2,1)S(1)}, bf16[2,256,1024]{2,1,0:T(8,128)(2,1)}, u32[]{:S(2)}) copy-start(bf16[2,256,1024]{2,1,0:T(8,128)(2,1)} %get-tuple-element.10) | copy-start | bytes 3145732
  124.9 5.7 %copy-start = (bf16[2,256,1024]{2,1,0:T(8,128)(2,1)S(1)}, bf16[2,256,1024]{2,1,0:T(8,128)(2,1)}, u32[]{:S(2)}) copy-start(bf16[2,256,1024]{2,1,0:T(8,128)(2,1)} %get-tuple-element.11) | copy-start | bytes 3145732

commit v3 on v2

v3 whole, which is shorter than its diff:
```python
import functools
import math

import jax
import jax.numpy as jnp
from jax import lax
from jax.experimental import pallas as pl
from jax.experimental.pallas import tpu as pltpu
from jax.sharding import PartitionSpec as P

HEAD_DIM = 128
GROUP = 2
MESH = pl.DeviceIdType.MESH
F32 = jnp.float32
BF16 = jnp.bfloat16
LOW = -1e30
TILE = 32
AHEAD = 3
LAG = 2


def dot_nt(a, b):
    return lax.dot_general(a, b, (((1,), (1,)), ((), ())), preferred_element_type=F32)


def dot_nn(a, b):
    return lax.dot_general(a, b, (((1,), (0,)), ((), ())), preferred_element_type=F32)


def dot_tn(a, b):
    return lax.dot_general(a, b, (((0,), (0,)), ((), ())), preferred_element_type=F32)


def kernel(
    levels, q_in, k_in, v_in, og_in, w_in, lo_out, dq_out, dk_out, dv_out,
    kv, qd, far, w, og, og_far, attn, s, p, dp, ds, top, norm, acc, own, dq, po, po_far, lo, st, st_far,
    ld_q, ld_kv, ld_og, ld_w, og_send, og_recv, po_send, po_recv,
    kv_send, kv_recv, do_send, do_recv, st_send, st_recv, out_sem, grad_sem,
):
    me = lax.axis_index("seq")
    hd = lax.axis_index("head")
    chunks, _, rows, width = kv.shape
    batch = og.shape[0]
    half = og.shape[2]
    per = chunks // batch
    scale = HEAD_DIM ** -0.5
    rate = scale * math.log2(math.e)
    own_cols = pl.multiple_of(hd * half, half)
    far_cols = pl.multiple_of((1 - hd) * half, half)

    def bit(j):
        return lax.rem(lax.shift_right_logical(me, j), 2)

    def partner(j):
        return me + (1 - 2 * bit(j)) * (1 << j)

    def cols(c):
        return pl.ds(pl.multiple_of(lax.rem(c, per) * width, width), width)

    def load_kv(c, i):
        src = (k_in, v_in)[i].at[lax.div(c, per), :, cols(c)]
        return pltpu.make_async_copy(src, kv.at[c, i], ld_kv.at[c, i])

    def load_q(c):
        return pltpu.make_async_copy(q_in.at[lax.div(c, per), :, cols(c)], qd.at[c, 0], ld_q.at[c])

    def load_og(b):
        return pltpu.make_async_copy(og_in.at[b], og.at[b], ld_og.at[b])

    load_w = pltpu.make_async_copy(w_in, w, ld_w)

    def to_head(src, dst, send, recv):
        return pltpu.make_async_remote_copy(
            src, dst, send, recv, device_id=(me, 1 - hd), device_id_type=MESH)

    def to_partner(j, src, dst, send, recv):
        return pltpu.make_async_remote_copy(
            src, dst, send, recv, device_id=(partner(j), hd), device_id_type=MESH)

    def send_og(b):
        return to_head(og_in.at[b], og_far.at[b], og_send.at[b], og_recv.at[b])

    def send_po(b):
        return to_head(po.at[b], po_far.at[b], po_send.at[b], po_recv.at[b])

    def send_kv(j, c):
        return to_partner(j, kv.at[c], far.at[j, c], kv_send.at[j, c], kv_recv.at[j, c])

    def send_q(j, c):
        return to_partner(j, qd.at[c, 0], far.at[j, c, 0], kv_send.at[j, c], kv_recv.at[j, c])

    def send_do(j, c):
        return to_partner(j, qd.at[c, 1], far.at[j, c, 1], do_send.at[j, c], do_recv.at[j, c])

    def send_st(j, c):
        return to_partner(j, st.at[c], st_far.at[j, c], st_send.at[j, c], st_recv.at[j, c])

    def put_dq(c):
        return pltpu.make_async_copy(dq.at[c], dq_out.at[lax.div(c, per), :, cols(c)], out_sem.at[c])

    def put_grad(c, i):
        dst = (dk_out, dv_out)[i].at[lax.div(c, per), :, cols(c)]
        return pltpu.make_async_copy(kv.at[c, i], dst, grad_sem.at[c, i])

    def start_loads(c, carry):
        load_kv(c, 0).start()
        load_kv(c, 1).start()
        load_q(c).start()
        return carry

    lax.fori_loop(0, chunks, start_loads, 0)
    for b in range(batch):
        load_og(b).start()
    load_w.start()

    barrier = pltpu.get_barrier_semaphore()
    for j in range(levels):
        pl.semaphore_signal(barrier, inc=1, device_id=(partner(j), hd), device_id_type=MESH)
    pl.semaphore_signal(barrier, inc=1, device_id=(me, 1 - hd), device_id_type=MESH)
    st[...] = jnp.zeros_like(st)
    pl.semaphore_wait(barrier, levels + 1)

    heads = [slice(u * HEAD_DIM, (u + 1) * HEAD_DIM) for u in range(GROUP)]
    tiles = [slice(t, t + TILE) for t in range(0, rows, TILE)]

    def issue(c):
        load_kv(c, 0).wait()
        load_kv(c, 1).wait()
        load_q(c).wait()
        for j in range(levels):
            @pl.when(bit(j) == 0)
            def _():
                send_kv(j, c).start()

            @pl.when(bit(j) == 1)
            def _():
                send_q(j, c).start()

    def issue_do(c):
        b = lax.div(c, per)

        @pl.when(lax.rem(c, per) == 0)
        def _():
            send_og(b).wait_recv()

        w_rows = pl.ds(pl.multiple_of(lax.rem(c, per) * width, width), width)
        qd[c, 1] = (
            dot_nt(og[b], w[w_rows, pl.ds(own_cols, half)])
            + dot_nt(og_far[b], w[w_rows, pl.ds(far_cols, half)])
        ).astype(BF16)
        for j in range(levels):
            @pl.when(bit(j) == 1)
            def _():
                send_do(j, c).start()

    send_og(0).start()

    def start_sends(c, carry):
        issue(c)
        if batch > 1:
            @pl.when(c == min(1, AHEAD - 1))
            def _():
                for b in range(1, batch):
                    send_og(b).start()
        return carry

    lax.fori_loop(0, AHEAD, start_sends, 0)
    for b in range(batch):
        load_og(b).wait()
    load_w.wait()
    lax.fori_loop(0, AHEAD, lambda c, carry: (issue_do(c), carry)[1], 0)

    def absorb(slot, u):
        peak = s[slot, u, tiles[0], :]
        for t in tiles[1:]:
            peak = jnp.maximum(peak, s[slot, u, t, :])
        old = top[u]
        new = jnp.maximum(old, jnp.max(peak, axis=0, keepdims=True))
        total = None
        for t in tiles:
            e = jnp.exp2((s[slot, u, t, :] - new) * rate)
            total = e if total is None else total + e
        norm[u] = norm[u] * jnp.exp2((old - new) * rate) + jnp.sum(total, axis=0, keepdims=True)
        top[u] = new

    def weigh(slot, u, c, value_ref):
        shift = norm[u]
        dp[slot, u] = dot_nt(value_ref[:, heads[u]], qd[c, 1, :, heads[u]])
        for t in tiles:
            e = jnp.exp2(s[slot, u, t, :] * rate - shift)
            s[slot, u, t, :] = e
            p[slot, u, t, :] = e.astype(BF16)
        acc[u] += dot_tn(value_ref[:, heads[u]], p[slot, u])

    def back(slot, u, key_ref):
        dsum = norm[u]
        for t in tiles:
            ds[u, t, :] = (s[slot, u, t, :] * (dp[slot, u, t, :] - dsum)).astype(BF16)
        acc[u] += dot_tn(key_ref[:, heads[u]], ds[u])

    def lower(c):
        k = lax.rem(c, LAG + 1)

        def one(j, carry):
            @pl.when(bit(j) == 0)
            def _():
                send_q(j, c).wait_recv()
                send_do(j, c).wait_recv()
                send_st(j, c).wait_recv()
                for u in range(GROUP):
                    s[j, u] = dot_nt(kv[c, 0, :, heads[u]], far[j, c, 0, :, heads[u]])
                    dp[j, u] = dot_nt(kv[c, 1, :, heads[u]], far[j, c, 1, :, heads[u]])
                for u in range(GROUP):
                    shift = st_far[j, c, u:u + 1, :]
                    dsum = st_far[j, c, GROUP + u:GROUP + u + 1, :]
                    for t in tiles:
                        e = jnp.exp2(s[j, u, t, :] * rate - shift)
                        p[j, u, t, :] = e.astype(BF16)
                        ds[u, t, :] = (e * (dp[j, u, t, :] - dsum)).astype(BF16)
                    own[k, 1, :, heads[u]] += dot_nn(p[j, u], far[j, c, 1, :, heads[u]])
                    own[k, 0, :, heads[u]] += dot_nn(ds[u], far[j, c, 0, :, heads[u]])
            return carry

        lax.fori_loop(0, levels, one, 0)
        for j in range(levels):
            @pl.when(bit(j) == 0)
            def _():
                send_kv(j, c).wait_send()
        for t in tiles:
            kv[c, 0, t, :] = (own[k, 0, t, :] * scale).astype(BF16)
            kv[c, 1, t, :] = own[k, 1, t, :].astype(BF16)
        for i in range(2):
            put_grad(c, i).start()

    def per_chunk(c, carry):
        b = lax.div(c, per)
        k = lax.rem(c, LAG + 1)
        for u in range(GROUP):
            top[u] = jnp.full((1, rows), LOW, F32)
            norm[u] = jnp.zeros((1, rows), F32)
            s[levels, u] = dot_nt(kv[c, 0, :, heads[u]], qd[c, 0, :, heads[u]])
        for u in range(GROUP):
            for t in tiles:
                at = lax.broadcasted_iota(jnp.int32, (TILE, rows), 0) + t.start
                to = lax.broadcasted_iota(jnp.int32, (TILE, rows), 1)
                s[levels, u, t, :] = jnp.where(at <= to, s[levels, u, t, :], LOW)
            absorb(levels, u)

        def score(j, carry):
            @pl.when(bit(j) == 1)
            def _():
                send_kv(j, c).wait_recv()
                for u in range(GROUP):
                    s[j, u] = dot_nt(far[j, c, 0, :, heads[u]], qd[c, 0, :, heads[u]])
                for u in range(GROUP):
                    absorb(j, u)
            return carry

        lax.fori_loop(0, levels, score, 0)

        for u in range(GROUP):
            norm[u] = top[u] * rate + jnp.log2(norm[u])
            st[c, u:u + 1, :] = norm[u]
            acc[u] = jnp.zeros((HEAD_DIM, rows), F32)
        for u in range(GROUP):
            weigh(levels, u, c, kv.at[c, 1])

        def weighted(j, carry):
            @pl.when(bit(j) == 1)
            def _():
                for u in range(GROUP):
                    weigh(j, u, c, far.at[j, c, 1])
            return carry

        lax.fori_loop(0, levels, weighted, 0)

        for u in range(GROUP):
            mixed = acc[u].astype(BF16).astype(F32)
            lean = qd[c, 1, :, heads[u]].astype(F32).T
            norm[u] = jnp.sum(mixed * lean, axis=0, keepdims=True)
            st[c, GROUP + u:GROUP + u + 1, :] = norm[u]
            at = pl.multiple_of(lax.rem(c, per) * width, width) + u * HEAD_DIM
            attn[b, :, pl.ds(pl.multiple_of(at, HEAD_DIM), HEAD_DIM)] = mixed.T.astype(BF16)
            acc[u] = jnp.zeros((HEAD_DIM, rows), F32)
        for j in range(levels):
            @pl.when(bit(j) == 1)
            def _():
                send_st(j, c).start()

        @pl.when(c + AHEAD < chunks)
        def _():
            issue(c + AHEAD)
            issue_do(c + AHEAD)

        @pl.when(lax.rem(c, per) == per - 1)
        def _():
            for t in range(0, half, width):
                at = pl.ds(pl.multiple_of(far_cols + t, width), width)
                po[b, :, t:t + width] = dot_nn(attn[b], w[:, at]).astype(BF16)
            send_po(b).start()
            for t in range(0, half, width):
                at = pl.ds(pl.multiple_of(own_cols + t, width), width)
                lo[b, :, t:t + width] = dot_nn(attn[b], w[:, at])

        for u in range(GROUP):
            back(levels, u, kv.at[c, 0])
            own[k, 0, :, heads[u]] = dot_nn(ds[u], qd[c, 0, :, heads[u]])
            own[k, 1, :, heads[u]] = dot_nn(p[levels, u], qd[c, 1, :, heads[u]])

        def backward(j, carry):
            @pl.when(bit(j) == 1)
            def _():
                for u in range(GROUP):
                    back(j, u, far.at[j, c, 0])
            return carry

        lax.fori_loop(0, levels, backward, 0)
        for u in range(GROUP):
            dq[c, :, heads[u]] = (acc[u] * scale).T.astype(BF16)
        put_dq(c).start()

        @pl.when(c >= LAG)
        def _():
            lower(c - LAG)
        return carry

    lax.fori_loop(0, chunks, per_chunk, 0)
    lax.fori_loop(chunks - LAG, chunks, lambda c, carry: (lower(c), carry)[1], 0)

    outs = []
    for b in range(batch):
        send_po(b).wait_recv()
        send_og(b).wait_send()
        for t in tiles:
            og[b, t, :] = (lo[b, t, :] + po_far[b, t, :].astype(F32)).astype(BF16)
        copy = pltpu.make_async_copy(og.at[b], lo_out.at[b], ld_og.at[b])
        copy.start()
        outs.append(copy)

    def drain(c, carry):
        put_dq(c).wait()
        put_grad(c, 0).wait()
        put_grad(c, 1).wait()
        for j in range(levels):
            @pl.when(bit(j) == 1)
            def _():
                send_q(j, c).wait_send()
                send_do(j, c).wait_send()
                send_st(j, c).wait_send()
        return carry

    lax.fori_loop(0, chunks, drain, 0)
    for b in range(batch):
        send_po(b).wait_send()
        outs[b].wait()


def solution(mesh):
    levels = mesh.shape["seq"].bit_length() - 1

    def step(queries, key_states, value_states, output_grad, out_proj):
        batch, rows, half = queries.shape
        width = GROUP * HEAD_DIM
        chunks = batch * (half // width)
        shape = jax.ShapeDtypeStruct(queries.shape, BF16)
        hbm = pl.BlockSpec(memory_space=pl.ANY)
        dma = pltpu.SemaphoreType.DMA
        return tuple(pl.pallas_call(
            functools.partial(kernel, levels),
            name="butterfly",
            out_shape=[shape] * 4,
            in_specs=[hbm] * 5,
            out_specs=[hbm] * 4,
            scratch_shapes=[
                pltpu.VMEM((chunks, 2, rows, width), BF16),
                pltpu.VMEM((chunks, 2, rows, width), BF16),
                pltpu.VMEM((levels, chunks, 2, rows, width), BF16),
                pltpu.VMEM(out_proj.shape, BF16),
                pltpu.VMEM((batch, rows, half), BF16),
                pltpu.VMEM((batch, rows, half), BF16),
                pltpu.VMEM((batch, rows, half), BF16),
                pltpu.VMEM((levels + 1, GROUP, rows, rows), F32),
                pltpu.VMEM((levels + 1, GROUP, rows, rows), BF16),
                pltpu.VMEM((levels + 1, GROUP, rows, rows), F32),
                pltpu.VMEM((GROUP, rows, rows), BF16),
                pltpu.VMEM((GROUP, 1, rows), F32),
                pltpu.VMEM((GROUP, 1, rows), F32),
                pltpu.VMEM((GROUP, HEAD_DIM, rows), F32),
                pltpu.VMEM((LAG + 1, 2, rows, width), F32),
                pltpu.VMEM((chunks, rows, width), BF16),
                pltpu.VMEM((batch, rows, half), BF16),
                pltpu.VMEM((batch, rows, half), BF16),
                pltpu.VMEM((batch, rows, half), F32),
                pltpu.VMEM((chunks, 8, rows), F32),
                pltpu.VMEM((levels, chunks, 8, rows), F32),
                dma((chunks,)),
                dma((chunks, 2)),
                dma((batch,)),
                dma,
                dma((batch,)),
                dma((batch,)),
                dma((batch,)),
                dma((batch,)),
                dma((levels, chunks)),
                dma((levels, chunks)),
                dma((levels, chunks)),
                dma((levels, chunks)),
                dma((levels, chunks)),
                dma((levels, chunks)),
                dma((chunks,)),
                dma((chunks, 2)),
            ],
            compiler_params=pltpu.CompilerParams(
                collective_id=0, has_side_effects=True, vmem_limit_bytes=60 << 20
            ),
        )(queries, key_states, value_states, output_grad, out_proj))

    act = P(None, "seq", "head")
    return jax.shard_map(
        step, mesh=mesh, in_specs=(act, act, act, act, P("head", None)),
        out_specs=(act,) * 4, check_vma=False,
    )
```

time: 133 us -> 121 us (0.910)
  the two profiles are of different devices: /device:TPU:14 before, /device:TPU:92 now
where the time goes in v3:
time: 121 us
  Pallas kernels  114 us (94%)
  local copies, waits for them, and re-layouts  6.62 us (5%)
    pallas_call x1, Pallas kernels, step(): pl.pallas_call(functools.partial(kernel, levels), name='butterfly', out_s...  114 us
    unnamed x8, local copies, waits for them, and re-layouts  6.62 us

profile of v3, /device:TPU:92, one launch (start us, length us, event | category | flops | bytes accessed | tf_op | source)
XLA Modules:
  0.0 121.3 jit_solution(5219020220989769704)
XLA Ops:
  0.6 114.1 %butterfly.1 = (bf16[2,256,1024]{2,1,0:T(8,128)(2,1)}, bf16[2,256,1024]{2,1,0:T(8,128)(2,1)}, bf16[2,256,1024]{2,1,0:T(8,128)(2,1)}, bf16[2,256,1024]{2,1,0:T(8,128)(2,1)}) custom-call(bf16[2,256,1024]{2,1,0:T(8,128)(2,1)} %q_in.1, bf16[2,256,1024]{2,1,0:T(8,128)(2,1)} %k_in.1, bf16[2,256,1024]{2,1,0:T(8,128)(2,1)} %v_in.1, bf16[2,256,1024]{2,1,0:T(8,128)(2,1)} %og_in.1, ...), custom_call_target="tpu_custom_call" | custom-call | tf_op jit(solution)/shard_map/butterfly/pallas_call | solution.py:368
  114.7 0.0 copy-start.1
  114.7 0.0 copy-start
  114.7 2.4 %copy.13 = bf16[2,256,1024]{2,1,0:T(8,128)(2,1)} copy(bf16[2,256,1024]{2,1,0:T(8,128)(2,1)} %get-tuple-element.8) | data formatting | bytes 2097152
  117.1 2.3 %copy.14 = bf16[2,256,1024]{2,1,0:T(8,128)(2,1)} copy(bf16[2,256,1024]{2,1,0:T(8,128)(2,1)} %get-tuple-element.9) | data formatting | bytes 2097152
  119.4 0.0 copy-done.1
  119.4 1.0 copy.15
  120.4 0.0 copy-done
  120.4 1.0 copy.16
Async XLA Ops:
  114.7 4.7 %copy-start.1 = (bf16[2,256,1024]{2,1,0:T(8,128)(2,1)S(1)}, bf16[2,256,1024]{2,1,0:T(8,128)(2,1)}, u32[]{:S(2)}) copy-start(bf16[2,256,1024]{2,1,0:T(8,128)(2,1)} %get-tuple-element.10) | copy-start | bytes 3145732
  114.7 5.7 %copy-start = (bf16[2,256,1024]{2,1,0:T(8,128)(2,1)S(1)}, bf16[2,256,1024]{2,1,0:T(8,128)(2,1)}, u32[]{:S(2)}) copy-start(bf16[2,256,1024]{2,1,0:T(8,128)(2,1)} %get-tuple-element.11) | copy-start | bytes 3145732

commit v4 on v3

--- a/solution.py
+++ b/solution.py
@@ -15,8 +15,11 @@
 BF16 = jnp.bfloat16
 LOW = -1e30
 TILE = 32
-AHEAD = 3
-LAG = 2
+RINGS = ((2, 3), (4, 5))
+AHEAD = 2
+AHEAD_KV = 8
+OG_AT = 1
+LAG = 3
 
 
 def dot_nt(a, b):
@@ -33,9 +36,9 @@
 
 def kernel(
     levels, q_in, k_in, v_in, og_in, w_in, lo_out, dq_out, dk_out, dv_out,
-    kv, qd, far, w, og, og_far, attn, s, p, dp, ds, top, norm, acc, own, dq, po, po_far, lo, st, st_far,
+    kv, qd, far, w, og, og_far, attn, s, p, dp, ds, top, norm, acc, own, po, po_far, lo, st, st_far,
     ld_q, ld_kv, ld_og, ld_w, og_send, og_recv, po_send, po_recv,
-    kv_send, kv_recv, do_send, do_recv, st_send, st_recv, out_sem, grad_sem,
+    kv_send, kv_recv, do_send, do_recv, st_send, st_recv, pass_send,
 ):
     me = lax.axis_index("seq")
     hd = lax.axis_index("head")
@@ -86,6 +89,34 @@
     def send_kv(j, c):
         return to_partner(j, kv.at[c], far.at[j, c], kv_send.at[j, c], kv_recv.at[j, c])
 
+    def passes(ring):
+        near, apart = RINGS[ring]
+        return (bit(near) == 1) & (bit(apart) == 0)
+
+    def opposite(ring):
+        near, apart = RINGS[ring]
+        return partner(near) + partner(apart) - me
+
+    def pass_kv(ring, c):
+        near, apart = RINGS[ring]
+        return pltpu.make_async_remote_copy(
+            far.at[near, c], far.at[apart, c], pass_send.at[ring, c], kv_recv.at[apart, c],
+            device_id=(opposite(ring), hd), device_id_type=MESH)
+
+    def pass_on(c):
+        for ring in range(len(RINGS)):
+            @pl.when(passes(ring))
+            def _():
+                send_kv(RINGS[ring][0], c).wait_recv()
+                pass_kv(ring, c).start()
+
+    def sends_own(j):
+        sender = bit(j) == 0
+        for near, apart in RINGS:
+            if j == apart:
+                sender = sender & (bit(near) == 1)
+        return sender
+
     def send_q(j, c):
         return to_partner(j, qd.at[c, 0], far.at[j, c, 0], kv_send.at[j, c], kv_recv.at[j, c])
 
@@ -94,13 +125,6 @@
 
     def send_st(j, c):
         return to_partner(j, st.at[c], st_far.at[j, c], st_send.at[j, c], st_recv.at[j, c])
-
-    def put_dq(c):
-        return pltpu.make_async_copy(dq.at[c], dq_out.at[lax.div(c, per), :, cols(c)], out_sem.at[c])
-
-    def put_grad(c, i):
-        dst = (dk_out, dv_out)[i].at[lax.div(c, per), :, cols(c)]
-        return pltpu.make_async_copy(kv.at[c, i], dst, grad_sem.at[c, i])
 
     def start_loads(c, carry):
         load_kv(c, 0).start()
@@ -116,22 +140,26 @@
     barrier = pltpu.get_barrier_semaphore()
     for j in range(levels):
         pl.semaphore_signal(barrier, inc=1, device_id=(partner(j), hd), device_id_type=MESH)
+    for ring in range(len(RINGS)):
+        pl.semaphore_signal(barrier, inc=1, device_id=(opposite(ring), hd), device_id_type=MESH)
     pl.semaphore_signal(barrier, inc=1, device_id=(me, 1 - hd), device_id_type=MESH)
     st[...] = jnp.zeros_like(st)
-    pl.semaphore_wait(barrier, levels + 1)
+    pl.semaphore_wait(barrier, levels + 1 + len(RINGS))
 
     heads = [slice(u * HEAD_DIM, (u + 1) * HEAD_DIM) for u in range(GROUP)]
     tiles = [slice(t, t + TILE) for t in range(0, rows, TILE)]
 
-    def issue(c):
+    def issue_kv(c):
         load_kv(c, 0).wait()
         load_kv(c, 1).wait()
+        for j in range(levels):
+            @pl.when(sends_own(j))
+            def _():
+                send_kv(j, c).start()
+
+    def issue(c):
         load_q(c).wait()
         for j in range(levels):
-            @pl.when(bit(j) == 0)
-            def _():
-                send_kv(j, c).start()
-
             @pl.when(bit(j) == 1)
             def _():
                 send_q(j, c).start()
@@ -156,15 +184,19 @@
     send_og(0).start()
 
     def start_sends(c, carry):
-        issue(c)
+        issue_kv(c)
+
+        @pl.when(c < AHEAD)
+        def _():
+            issue(c)
         if batch > 1:
-            @pl.when(c == min(1, AHEAD - 1))
+            @pl.when(c == OG_AT)
             def _():
                 for b in range(1, batch):
                     send_og(b).start()
         return carry
 
-    lax.fori_loop(0, AHEAD, start_sends, 0)
+    lax.fori_loop(0, AHEAD_KV, start_sends, 0)
     for b in range(batch):
         load_og(b).wait()
     load_w.wait()
@@ -199,6 +231,7 @@
         acc[u] += dot_tn(key_ref[:, heads[u]], ds[u])
 
     def lower(c):
+        b = lax.div(c, per)
         k = lax.rem(c, LAG + 1)
 
         def one(j, carry):
@@ -222,15 +255,9 @@
             return carry
 
         lax.fori_loop(0, levels, one, 0)
-        for j in range(levels):
-            @pl.when(bit(j) == 0)
-            def _():
-                send_kv(j, c).wait_send()
         for t in tiles:
-            kv[c, 0, t, :] = (own[k, 0, t, :] * scale).astype(BF16)
-            kv[c, 1, t, :] = own[k, 1, t, :].astype(BF16)
-        for i in range(2):
-            put_grad(c, i).start()
+            dk_out[b, t, cols(c)] = (own[k, 0, t, :] * scale).astype(BF16)
+            dv_out[b, t, cols(c)] = own[k, 1, t, :].astype(BF16)
 
     def per_chunk(c, carry):
         b = lax.div(c, per)
@@ -247,9 +274,16 @@
             absorb(levels, u)
 
         def score(j, carry):
-            @pl.when(bit(j) == 1)
+            held = False
+            for ring in range(len(RINGS)):
+                held = held | (passes(ring) & (j == RINGS[ring][0]))
+
+            @pl.when((bit(j) == 1) & jnp.logical_not(held))
             def _():
                 send_kv(j, c).wait_recv()
+
+            @pl.when(bit(j) == 1)
+            def _():
                 for u in range(GROUP):
                     s[j, u] = dot_nt(far[j, c, 0, :, heads[u]], qd[c, 0, :, heads[u]])
                 for u in range(GROUP):
@@ -257,6 +291,10 @@
             return carry
 
         lax.fori_loop(0, levels, score, 0)
+
+        @pl.when(c + 1 < chunks)
+        def _():
+            pass_on(c + 1)
 
         for u in range(GROUP):
             norm[u] = top[u] * rate + jnp.log2(norm[u])
@@ -316,31 +354,33 @@
 
         lax.fori_loop(0, levels, backward, 0)
         for u in range(GROUP):
-            dq[c, :, heads[u]] = (acc[u] * scale).T.astype(BF16)
-        put_dq(c).start()
+            at = pl.multiple_of(lax.rem(c, per) * width, width) + u * HEAD_DIM
+            at = pl.ds(pl.multiple_of(at, HEAD_DIM), HEAD_DIM)
+            dq_out[b, :, at] = (acc[u] * scale).T.astype(BF16)
 
         @pl.when(c >= LAG)
         def _():
             lower(c - LAG)
         return carry
 
+    pass_on(0)
     lax.fori_loop(0, chunks, per_chunk, 0)
     lax.fori_loop(chunks - LAG, chunks, lambda c, carry: (lower(c), carry)[1], 0)
 
-    outs = []
     for b in range(batch):
         send_po(b).wait_recv()
-        send_og(b).wait_send()
         for t in tiles:
-            og[b, t, :] = (lo[b, t, :] + po_far[b, t, :].astype(F32)).astype(BF16)
-        copy = pltpu.make_async_copy(og.at[b], lo_out.at[b], ld_og.at[b])
-        copy.start()
-        outs.append(copy)
+            lo_out[b, t, :] = (lo[b, t, :] + po_far[b, t, :].astype(F32)).astype(BF16)
 
     def drain(c, carry):
-        put_dq(c).wait()
-        put_grad(c, 0).wait()
-        put_grad(c, 1).wait()
+        for j in range(levels):
+            @pl.when(sends_own(j))
+            def _():
+                send_kv(j, c).wait_send()
+        for ring in range(len(RINGS)):
+            @pl.when(passes(ring))
+            def _():
+                pass_kv(ring, c).wait_send()
         for j in range(levels):
             @pl.when(bit(j) == 1)
             def _():
@@ -351,8 +391,8 @@
 
     lax.fori_loop(0, chunks, drain, 0)
     for b in range(batch):
+        send_og(b).wait_send()
         send_po(b).wait_send()
-        outs[b].wait()
 
 
 def solution(mesh):
@@ -362,7 +402,7 @@
         batch, rows, half = queries.shape
         width = GROUP * HEAD_DIM
         chunks = batch * (half // width)
-        shape = jax.ShapeDtypeStruct(queries.shape, BF16)
+        shape = pltpu.VMEM(queries.shape, BF16)
         hbm = pl.BlockSpec(memory_space=pl.ANY)
         dma = pltpu.SemaphoreType.DMA
         return tuple(pl.pallas_call(
@@ -370,7 +410,7 @@
             name="butterfly",
             out_shape=[shape] * 4,
             in_specs=[hbm] * 5,
-            out_specs=[hbm] * 4,
+            out_specs=[pl.BlockSpec(memory_space=pltpu.VMEM)] * 4,
             scratch_shapes=[
                 pltpu.VMEM((chunks, 2, rows, width), BF16),
                 pltpu.VMEM((chunks, 2, rows, width), BF16),
@@ -387,7 +427,6 @@
                 pltpu.VMEM((GROUP, 1, rows), F32),
                 pltpu.VMEM((GROUP, HEAD_DIM, rows), F32),
                 pltpu.VMEM((LAG + 1, 2, rows, width), F32),
-                pltpu.VMEM((chunks, rows, width), BF16),
                 pltpu.VMEM((batch, rows, half), BF16),
                 pltpu.VMEM((batch, rows, half), BF16),
                 pltpu.VMEM((batch, rows, half), F32),
@@ -407,11 +446,10 @@
                 dma((levels, chunks)),
                 dma((levels, chunks)),
                 dma((levels, chunks)),
-                dma((chunks,)),
-                dma((chunks, 2)),
+                dma((len(RINGS), chunks)),
             ],
             compiler_params=pltpu.CompilerParams(
-                collective_id=0, has_side_effects=True, vmem_limit_bytes=60 << 20
+                collective_id=0, has_side_effects=True, vmem_limit_bytes=119 << 19
             ),
         )(queries, key_states, value_states, output_grad, out_proj))
 

time: 121 us -> 113 us (0.934)
  the two profiles are of different devices: /device:TPU:92 before, /device:TPU:14 now
where the time goes in v4:
time: 113 us; the launch traced here: 111 us
  Pallas kernels  107 us (95%)
  local copies, waits for them, and re-layouts  3.88 us (3%)
    pallas_call x1, Pallas kernels, step(): pl.pallas_call(functools.partial(kernel, levels), name='butterfly', out_s...  107 us
    unnamed x4, local copies, waits for them, and re-layouts  3.88 us

profile of v4, /device:TPU:14, one launch (start us, length us, event | category | flops | bytes accessed | tf_op | source)
XLA Modules:
  0.0 111.5 jit_solution(5311772177131998958)
XLA Ops:
  0.6 107.0 %butterfly.1 = (bf16[2,256,1024]{2,1,0:T(8,128)(2,1)S(1)}, bf16[2,256,1024]{2,1,0:T(8,128)(2,1)S(1)}, bf16[2,256,1024]{2,1,0:T(8,128)(2,1)S(1)}, bf16[2,256,1024]{2,1,0:T(8,128)(2,1)S(1)}) custom-call(bf16[2,256,1024]{2,1,0:T(8,128)(2,1)} %q_in.1, bf16[2,256,1024]{2,1,0:T(8,128)(2,1)} %k_in.1, bf16[2,256,1024]{2,1,0:T(8,128)(2,1)} %v_in.1, ...), custom_call_target="tpu_custom_call" | custom-call | tf_op jit(solution)/shard_map/butterfly/pallas_call | solution.py:408
  107.6 1.0 copy.13
  108.6 1.0 copy.14
  109.6 1.0 copy.15
  110.5 1.0 copy.16

commit v5 on v4

--- a/solution.py
+++ b/solution.py
@@ -395,6 +395,16 @@
         send_po(b).wait_send()
 
 
+def put_out(a, b, c, d, a_out, b_out, c_out, d_out, sem):
+    copies = []
+    for i, (src, dst) in enumerate(((a, a_out), (b, b_out), (c, c_out), (d, d_out))):
+        for k in range(src.shape[0]):
+            copies.append(pltpu.make_async_copy(src.at[k], dst.at[k], sem.at[i, k]))
+            copies[-1].start()
+    for copy in copies:
+        copy.wait()
+
+
 def solution(mesh):
     levels = mesh.shape["seq"].bit_length() - 1
 
@@ -405,7 +415,7 @@
         shape = pltpu.VMEM(queries.shape, BF16)
         hbm = pl.BlockSpec(memory_space=pl.ANY)
         dma = pltpu.SemaphoreType.DMA
-        return tuple(pl.pallas_call(
+        results = pl.pallas_call(
             functools.partial(kernel, levels),
             name="butterfly",
             out_shape=[shape] * 4,
@@ -451,7 +461,16 @@
             compiler_params=pltpu.CompilerParams(
                 collective_id=0, has_side_effects=True, vmem_limit_bytes=119 << 19
             ),
-        )(queries, key_states, value_states, output_grad, out_proj))
+        )(queries, key_states, value_states, output_grad, out_proj)
+        return tuple(pl.pallas_call(
+            put_out,
+            name="put_out",
+            out_shape=[jax.ShapeDtypeStruct(queries.shape, BF16)] * 4,
+            in_specs=[pl.BlockSpec(memory_space=pltpu.VMEM)] * 4,
+            out_specs=[hbm] * 4,
+            scratch_shapes=[dma((4, batch))],
+            compiler_params=pltpu.CompilerParams(vmem_limit_bytes=1 << 20),
+        )(*results))
 
     act = P(None, "seq", "head")
     return jax.shard_map(

time: 113 us -> 112 us (level)
  local copies, waits for them, and re-layouts: 3.88 us -> 0 us
  Pallas kernels: 107 us -> 109 us
    unnamed x4 -> x0, local copies, waits for them, and re-layouts: 3.88 us -> none
    pallas_call x0 -> x1, Pallas kernels: none -> 2.07 us  [step(): pl.pallas_call(put_out, name='put_out', out_shape=[jax.ShapeDtypeStruct(q...]
where the time goes in v5:
time: 112 us; the launch traced here: 110 us
  Pallas kernels  109 us (97%)
    pallas_call x1, Pallas kernels, step(): pl.pallas_call(functools.partial(kernel, levels), name='butterfly', out_s...  107 us

profile of v5, /device:TPU:14, one launch (start us, length us, event | category | flops | bytes accessed | tf_op | source)
XLA Modules:
  0.0 109.7 jit_solution(7133677772336609835)
XLA Ops:
  0.6 107.0 %butterfly.1 = (bf16[2,256,1024]{2,1,0:T(8,128)(2,1)S(1)}, bf16[2,256,1024]{2,1,0:T(8,128)(2,1)S(1)}, bf16[2,256,1024]{2,1,0:T(8,128)(2,1)S(1)}, bf16[2,256,1024]{2,1,0:T(8,128)(2,1)S(1)}) custom-call(bf16[2,256,1024]{2,1,0:T(8,128)(2,1)} %q_in.1, bf16[2,256,1024]{2,1,0:T(8,128)(2,1)} %k_in.1, bf16[2,256,1024]{2,1,0:T(8,128)(2,1)} %v_in.1, ...), custom_call_target="tpu_custom_call" | custom-call | tf_op jit(solution)/shard_map/butterfly/pallas_call | solution.py:418
  107.6 2.1 %put_out.1 = (bf16[2,256,1024]{2,1,0:T(8,128)(2,1)}, bf16[2,256,1024]{2,1,0:T(8,128)(2,1)}, bf16[2,256,1024]{2,1,0:T(8,128)(2,1)}, bf16[2,256,1024]{2,1,0:T(8,128)(2,1)}) custom-call(bf16[2,256,1024]{2,1,0:T(8,128)(2,1)S(1)} %get-tuple-element.8.a, bf16[2,256,1024]{2,1,0:T(8,128)(2,1)S(1)} %get-tuple-element.9.b, ...), custom_call_target="tpu_custom_call" | custom-call | tf_op jit(solution)/shard_map/put_out/pallas_call | solution.py:465

commit v6 on v5

--- a/solution.py
+++ b/solution.py
@@ -83,8 +83,8 @@
     def send_og(b):
         return to_head(og_in.at[b], og_far.at[b], og_send.at[b], og_recv.at[b])
 
-    def send_po(b):
-        return to_head(po.at[b], po_far.at[b], po_send.at[b], po_recv.at[b])
+    def send_po(b, n):
+        return to_head(po.at[b, n], po_far.at[b, n], po_send.at[b, n], po_recv.at[b, n])
 
     def send_kv(j, c):
         return to_partner(j, kv.at[c], far.at[j, c], kv_send.at[j, c], kv_recv.at[j, c])
@@ -334,8 +334,8 @@
         def _():
             for t in range(0, half, width):
                 at = pl.ds(pl.multiple_of(far_cols + t, width), width)
-                po[b, :, t:t + width] = dot_nn(attn[b], w[:, at]).astype(BF16)
-            send_po(b).start()
+                po[b, t // width] = dot_nn(attn[b], w[:, at]).astype(BF16)
+                send_po(b, t // width).start()
             for t in range(0, half, width):
                 at = pl.ds(pl.multiple_of(own_cols + t, width), width)
                 lo[b, :, t:t + width] = dot_nn(attn[b], w[:, at])
@@ -365,12 +365,15 @@
 
     pass_on(0)
     lax.fori_loop(0, chunks, per_chunk, 0)
-    lax.fori_loop(chunks - LAG, chunks, lambda c, carry: (lower(c), carry)[1], 0)
-
+    lax.fori_loop(chunks - LAG, chunks - 1, lambda c, carry: (lower(c), carry)[1], 0)
     for b in range(batch):
-        send_po(b).wait_recv()
-        for t in tiles:
-            lo_out[b, t, :] = (lo[b, t, :] + po_far[b, t, :].astype(F32)).astype(BF16)
+        for n in range(half // width):
+            send_po(b, n).wait_recv()
+            at = slice(n * width, (n + 1) * width)
+            for t in tiles:
+                lo_out[b, t, at] = (lo[b, t, at] + po_far[b, n, t, :].astype(F32)).astype(BF16)
+
+    lower(chunks - 1)
 
     def drain(c, carry):
         for j in range(levels):
@@ -392,7 +395,8 @@
     lax.fori_loop(0, chunks, drain, 0)
     for b in range(batch):
         send_og(b).wait_send()
-        send_po(b).wait_send()
+        for n in range(half // width):
+            send_po(b, n).wait_send()
 
 
 def put_out(a, b, c, d, a_out, b_out, c_out, d_out, sem):
@@ -437,8 +441,8 @@
                 pltpu.VMEM((GROUP, 1, rows), F32),
                 pltpu.VMEM((GROUP, HEAD_DIM, rows), F32),
                 pltpu.VMEM((LAG + 1, 2, rows, width), F32),
-                pltpu.VMEM((batch, rows, half), BF16),
-                pltpu.VMEM((batch, rows, half), BF16),
+                pltpu.VMEM((batch, half // width, rows, width), BF16),
+                pltpu.VMEM((batch, half // width, rows, width), BF16),
                 pltpu.VMEM((batch, rows, half), F32),
                 pltpu.VMEM((chunks, 8, rows), F32),
                 pltpu.VMEM((levels, chunks, 8, rows), F32),
@@ -448,8 +452,8 @@
                 dma,
                 dma((batch,)),
                 dma((batch,)),
-                dma((batch,)),
-                dma((batch,)),
+                dma((batch, half // width)),
+                dma((batch, half // width)),
                 dma((levels, chunks)),
                 dma((levels, chunks)),
                 dma((levels, chunks)),

time: 112 us -> 112 us (level)
  no operation moved by 1% of the time
where the time goes in v6:
time: 112 us; the launch traced here: 110 us
  Pallas kernels  109 us (97%)
    pallas_call x1, Pallas kernels, step(): pl.pallas_call(functools.partial(kernel, levels), name='butterfly', out_s...  107 us

profile of v6, /device:TPU:14, one launch (start us, length us, event | category | flops | bytes accessed | tf_op | source)
XLA Modules:
  0.0 109.8 jit_solution(17825852024631506559)
XLA Ops:
  0.6 107.1 %butterfly.1 = (bf16[2,256,1024]{2,1,0:T(8,128)(2,1)S(1)}, bf16[2,256,1024]{2,1,0:T(8,128)(2,1)S(1)}, bf16[2,256,1024]{2,1,0:T(8,128)(2,1)S(1)}, bf16[2,256,1024]{2,1,0:T(8,128)(2,1)S(1)}) custom-call(bf16[2,256,1024]{2,1,0:T(8,128)(2,1)} %q_in.1, bf16[2,256,1024]{2,1,0:T(8,128)(2,1)} %k_in.1, bf16[2,256,1024]{2,1,0:T(8,128)(2,1)} %v_in.1, ...), custom_call_target="tpu_custom_call" | custom-call | tf_op jit(solution)/shard_map/butterfly/pallas_call | solution.py:422
  107.8 2.1 %put_out.1 = (bf16[2,256,1024]{2,1,0:T(8,128)(2,1)}, bf16[2,256,1024]{2,1,0:T(8,128)(2,1)}, bf16[2,256,1024]{2,1,0:T(8,128)(2,1)}, bf16[2,256,1024]{2,1,0:T(8,128)(2,1)}) custom-call(bf16[2,256,1024]{2,1,0:T(8,128)(2,1)S(1)} %get-tuple-element.8.a, bf16[2,256,1024]{2,1,0:T(8,128)(2,1)S(1)} %get-tuple-element.9.b, ...), custom_call_target="tpu_custom_call" | custom-call | tf_op jit(solution)/shard_map/put_out/pallas_call | solution.py:469
